TPU v7x, 256 devices: a whole 4x4x8 slice. The times are simulated.
256 devices in a mesh: front: 64 (over z, x, core), col: 4 (over y).
Axes of the slice: x: 4, y: 4, z: 8, core: 2. Of those that a mesh axis runs over, the one named last changes fastest.
Arguments:
- leaf_load: bfloat16 [65536, 2048], P('front', 'col'), may hold values from -6 to 6
- leaf_inverse: bfloat16 [65536, 1024], P(('front', 'col')), may hold values from -0.1875 to 0.1875
- leaf_coupling: bfloat16 [32768, 1024], P('front'), may hold values from -0.1875 to 0.1875
- leaf_rowmap: int32 [64, 512], P('front'), may hold values from 0 to 511, each once within a row
- load_first: bfloat16 [16384, 2048], P('front', 'col'), may hold values from -6 to 6
- load_second: bfloat16 [8192, 2048], P('front', 'col'), may hold values from -6 to 6
- load_third: bfloat16 [4096, 2048], P('front', 'col'), may hold values from -6 to 6
- inverse_first: bfloat16 [16384, 512], P('front'), may hold values from -0.15625 to 0.15625
- inverse_second: bfloat16 [8192, 512], P('front'), may hold values from -0.15625 to 0.15625
- inverse_third: bfloat16 [4096, 512], P('front'), may hold values from -0.15625 to 0.15625
- coupling_first: bfloat16 [512, 16384], P(None, 'front'), may hold values from -0.25 to 0.25
- coupling_second: bfloat16 [512, 8192], P(None, 'front'), may hold values from -0.25 to 0.25
- rowmap_first: int32 [32, 512], replicated, may hold values from 0 to 511, each once within a row
- rowmap_second: int32 [16, 512], replicated, may hold values from 0 to 511, each once within a row
- surface_coupling: bfloat16 [192, 1024, 1024], P('front'), may hold values from -0.125 to 0.125
- neighbor_tiles: int32 [64, 2], replicated, may hold values from 0 to 63, as said below
Outputs:
- volume_solution: bfloat16 [65536, 2048], P('front', 'col')
- surface_tiles: bfloat16 [65536, 2048], P('front', 'col')
- solution_first: bfloat16 [16384, 2048], P('front', 'col')
- solution_second: bfloat16 [8192, 2048], P('front', 'col')
- solution_third: bfloat16 [4096, 2048], P('front', 'col')
Inputs may be any that keep to these rules, and one draw needn't show every extreme that they name: Each row of leaf_rowmap is a permutation of the 512 separator rows. Each row of rowmap_first is a permutation of the 512 separator rows. Each row of rowmap_second is a permutation of the 512 separator rows. `neighbor_tiles`: row f names two different tiles, neither equal to f, each within 2 of f; counting each front's own tile, every tile receives 1 to 5 contributions, and some tile receives 5.
All inputs are finite; a program needn't handle non-finite values.
Results may differ from a plain program's by a relative error of at most 0.015.
Values may be sent and summed in bfloat16 or wider, within the bound.
No kernel may reach another device: no remote copies, remote signals or barrier semaphores. Data moves between devices by JAX's collectives and lax.ppermute only.
A program may use at most 128 MiB of HBM per device.

v0:
```python
import functools

import jax
import jax.numpy as jnp
from jax import lax
from jax.experimental import pallas as pl
from jax.experimental.pallas import tpu as pltpu
from jax.sharding import PartitionSpec as P

F32 = jnp.float32
BF16 = jnp.bfloat16


def flip(x, mask):
    count = lax.axis_size("front")
    return lax.ppermute(x, "front", [(i, i ^ mask) for i in range(count)])


def shift(x, axis, steps):
    count = lax.axis_size(axis)
    return lax.ppermute(x, axis, [(i, (i + steps) % count) for i in range(count)])


def pass_on(x, axis, steps):
    count = lax.axis_size(axis)
    return lax.ppermute(x, axis, [(i, i + steps) for i in range(count) if 0 <= i + steps < count])


def mm(a, b):
    return jnp.dot(a, b, preferred_element_type=F32)


def mm_t(a, b):
    return lax.dot_general(a, b, (((0,), (0,)), ((), ())), preferred_element_type=F32)


class Held:
    def __init__(self, source, target, sem):
        self.copy = pltpu.make_async_copy(source, target, sem)
        self.target = target
        self.shape = target.shape
        self.copy.start()

    def wait(self):
        self.copy.wait()

    def __getitem__(self, index):
        return self.target[index]


def kernel(body, outs, args, flops=1e9, fetched=(), scalars=(), scratch=()):
    vmem = pl.BlockSpec(memory_space=pltpu.VMEM)
    specs = [pl.BlockSpec(memory_space=pltpu.HBM) if i in fetched else vmem for i in range(len(args))]
    nbytes = sum(a.size * a.dtype.itemsize for a in args)
    order = sorted(fetched)
    shapes = [cut_shape(fetched, i, args[i]) for i in order]

    def run(*refs):
        ins, rest = list(refs[: len(args)]), refs[len(args) :]
        numbers, rest = rest[: len(scalars)], rest[len(scalars) :]
        results, rest = rest[: len(outs)], rest[len(outs) :]
        own, rest = rest[: len(scratch)], rest[len(scratch) :]
        for k, i in enumerate(order):
            source = ins[i]
            if isinstance(fetched, dict) and fetched[i]:
                source = source.at[fetched[i]]
            ins[i] = Held(source, rest[k], rest[len(order)].at[k])
        body(*ins, *numbers, *results, *own)

    extra = [pltpu.VMEM(shape, args[i].dtype) for i, shape in zip(order, shapes)]
    if order:
        extra.append(pltpu.SemaphoreType.DMA((len(order),)))
    args = [pltpu.with_memory_space_constraint(a, pltpu.HBM) if i in fetched else a for i, a in enumerate(args)]
    return pl.pallas_call(
        run,
        out_shape=[jax.ShapeDtypeStruct(s, t) for s, t in outs],
        in_specs=specs + [pl.BlockSpec(memory_space=pltpu.SMEM)] * len(scalars),
        out_specs=[vmem] * len(outs),
        scratch_shapes=list(scratch) + extra,
        compiler_params=pltpu.CompilerParams(vmem_limit_bytes=10 << 20),
        cost_estimate=pl.CostEstimate(flops=int(flops), bytes_accessed=nbytes, transcendentals=0),
    )(*args, *scalars)


def cut_shape(fetched, i, array):
    cut = fetched[i] if isinstance(fetched, dict) else None
    if not cut:
        return array.shape
    return tuple(len(range(*c.indices(n))) for c, n in zip(cut, array.shape, strict=True))


def block(i, size):
    return pl.ds(pl.multiple_of(i * size, size), size)


def each(count, size, step):
    lax.fori_loop(0, count // size, lambda i, carry: (step(block(i, size)), carry)[1], 0)


def selector_t(row_map):
    order = row_map.shape[1]
    return (row_map == lax.broadcasted_iota(jnp.int32, (order, order), 0)).astype(BF16)


def pack_body(rm1, rm2, d_own, e_own, inv1, inv2, inv3, load2, load3, aimed, out_x, out_c, out_aim):
    front = lax.axis_index("front")
    n2, n3 = inv2.shape[0], inv3.shape[0]
    for x in (rm1, rm2, d_own, e_own, inv1, inv2, inv3, load2, load3):
        x.wait()
    select = selector_t(rm2[pl.ds(front >> 2, 1), :])
    e_t = mm_t(e_own[...], select).astype(BF16)
    out_x[:n2, :] = inv2[...]
    out_x[n2 : 2 * n2, :] = e_t
    out_x[2 * n2 : 2 * n2 + n3, :] = inv3[...]
    out_x[2 * n2 + n3 :, :] = load3[...]
    select = selector_t(rm1[pl.ds(front >> 1, 1), :])
    n1 = inv1.shape[0]
    out_c[:n1, :] = mm_t(d_own[...], select).astype(BF16)
    out_c[n1 : 2 * n1, :] = inv1[...]
    out_c[2 * n1 :, :] = load2[...]
    row = lax.broadcasted_iota(jnp.int32, out_aim.shape, 0)
    out_aim[...] = jnp.where(row == 0, aimed[front, 0] - front, aimed[front, 1] - front)


def leaf_weight_body(rm, c, out_c, out_ct):
    select = selector_t(rm[...])
    size = 256

    def step(i, carry):
        cols = block(i, size)
        own = c[:, cols]
        out_c[:, cols] = mm_t(select, own).astype(BF16)
        out_ct[cols, :] = mm_t(own, select).astype(BF16)
        return carry

    lax.fori_loop(0, c.shape[1] // size, step, 0)


def leaf_term(pieces, columns, c, size):
    col = lax.axis_index("col")
    total = 0.0
    for piece, place in pieces:
        cols = pl.ds(pl.multiple_of(((2 * col + place) & 7) * size, size), piece.shape[0])
        total = total + mm(c[:, cols], mm(piece[...], columns).astype(BF16))
    return total


def near_body(own, up_top, down_low, b, c, load1, out_other, out_mine):
    core = lax.axis_index("front") & 1
    half, size = b.shape[1] // 2, up_top.shape[0]
    for out, which in ((out_other, 1 - core), (out_mine, core)):
        out[...] = -leaf_term(((own, 0), (up_top, 6), (down_low, 3)), b[:, block(which, half)], c, size)
        rows = block(core, load1.shape[0])
        out[rows, :] += load1[:, block(which, half)].astype(F32)


def far_term(up_low, down_top, far_top, far_low, b, c, near, which):
    half, size = b.shape[1] // 2, far_top.shape[0]
    pieces = ((up_low, 7), (down_top, 2), (far_top, 4), (far_low, 5))
    return near[...] - leaf_term(pieces, b[:, block(which, half)], c, size)


def other_body(up_low, down_top, far_top, far_low, b, c, near, out):
    core = lax.axis_index("front") & 1
    out[...] = far_term(up_low, down_top, far_top, far_low, b, c, near, 1 - core).astype(BF16)


def mine_body(up_low, down_top, far_top, far_low, b, c, near, out):
    core = lax.axis_index("front") & 1
    out[...] = far_term(up_low, down_top, far_top, far_low, b, c, near, core)


def first_weight_body(pack, away, load_half, out_d, out_dt, out_inv, out_load):
    front = lax.axis_index("front")
    core = front & 1
    n1 = out_inv.shape[0] // 2
    n2 = away.shape[0] - 2 * n1
    half = out_load.shape[1]
    out_load[...] = jnp.zeros_like(out_load)
    for piece, place in ((pack, core), (away, 1 - core)):
        rows = block(place, n1)
        t = piece[:n1, :]
        out_dt[rows, :] = t
        out_d[:, rows] = t.T
        out_inv[rows, :] = piece[n1 : 2 * n1, :]
        where = block(2 * ((front >> 1) & 1) + place, n2)
        out_load[where, :] = piece[2 * n1 :, block(core, half)]


def second_weight_body(p0, p1, p2, p3, out_e, out_et, out_inv, out_load, out_third):
    front = lax.axis_index("front")
    core = front & 1
    n2 = out_inv.shape[0] // 4
    n3 = n2 // 2
    half = out_load.shape[1]
    out_load[...] = jnp.zeros_like(out_load)
    for mask, piece in enumerate((p0, p1, p2, p3)):
        place = (front & 3) ^ mask
        rows = block(place, n2)
        t = piece[n2 : 2 * n2, :]
        out_inv[rows, :] = piece[:n2, :]
        out_et[rows, :] = t
        out_e[:, rows] = t.T
        out_third[block(place, n3), :] = piece[2 * n2 : 2 * n2 + n3, :]
        out_load[block(((front >> 2) & 1) * 4 + place, n3), :] = piece[2 * n2 + n3 :, block(core, half)]


def first_body(mine, other, inv, d, load2, out_rhs, out_term):
    rhs = (mine[...].astype(F32) + other[...].astype(F32)).astype(BF16)
    out_rhs[...] = rhs
    y = mm(inv[...], rhs).astype(BF16)
    out_term[...] = (load2[...].astype(F32) - mm(d[...], y)).astype(BF16)


def second_body(mine, other, inv, e, load3, out_rhs, out_term):
    first_body(mine, other, inv, e, load3, out_rhs, out_term)


def down_body(mine, other, third_near, third_far, e_t, inv2, rhs2, d_t, inv1, rhs1, out1, own2, away2, own3, away3, out3, out2):
    front = lax.axis_index("front")
    bit = (front >> 2) & 1
    rhs = (mine[...].astype(F32) + other[...].astype(F32)).astype(BF16)
    rows = third_near.shape[0]
    out3[block(bit, rows), :] = mm(third_near[...], rhs).astype(BF16)
    out3[block(1 - bit, rows), :] = mm(third_far[...], rhs).astype(BF16)
    left = (rhs2[...].astype(F32) - mm(e_t[...], out3[...])).astype(BF16)
    sol = mm(inv2[...], left).astype(BF16)
    out2[...] = sol
    left = (rhs1[...].astype(F32) - mm(d_t[...], sol)).astype(BF16)
    out1[...] = mm(inv1[...], left).astype(BF16)
    for own, away, whole, place in ((own2, away2, out2, front & 3), (own3, away3, out3, front & 7)):
        own[...] = whole[block(place, own.shape[0]), :]
        away[...] = whole[block(place ^ 1, own.shape[0]), :]


def stage_body(c_t, b, surface, own, up_top, up_low, down_top, down_low, far_top, far_low, out_ct, out_b, out_surface, out_factor, sems):
    col = lax.axis_index("col")
    size = up_top.shape[0]
    pairs = [(c_t, out_ct), (b, out_b)]
    for piece, place in ((own, 0), (up_top, 6), (up_low, 7), (down_top, 2), (down_low, 3), (far_top, 4), (far_low, 5)):
        rows = pl.ds(pl.multiple_of(((2 * col + place) & 7) * size, size), piece.shape[0])
        pairs.append((piece, out_factor.at[rows, :]))
    pairs.append((surface, out_surface))
    copies = [pltpu.make_async_copy(x, y, sems.at[i]) for i, (x, y) in enumerate(pairs)]
    for copy in copies:
        copy.start()
    for copy in copies:
        copy.wait()


def volume_body(part, c_t, b, factor, surface, s_own, s_away, aim, *rest):
    out, out_v, out_near, out_relay, out_up, out_down, left, sem = rest[-8:]
    front = lax.axis_index("front")
    core = front & 1
    half = out_v.shape[1]
    side = jnp.where(core == part, s_own[...], s_away[...])

    def start(rows):
        left[rows, :] = (b[rows, part * half : (part + 1) * half].astype(F32) - mm(c_t[rows, :], side)).astype(BF16)

    def solve(rows):
        out_v[rows, :] = mm(factor[rows, :], left[...]).astype(BF16)

    each(b.shape[0], 256, start)
    each(b.shape[0], 256, solve)
    store = pltpu.make_async_copy(out_v, out.at[:, part * half : (part + 1) * half], sem)
    store.start()
    inner = 1 - 2 * core

    def tiles(rows):
        v = out_v[...]
        c_one = mm(surface[1, rows, :], v).astype(BF16)
        c_two = mm(surface[2, rows, :], v).astype(BF16)
        zero = jnp.zeros_like(c_one)
        one = jnp.broadcast_to(aim[0:1, 0:1], c_one.shape)
        two = jnp.broadcast_to(aim[1:2, 0:1], c_one.shape)
        for out, offset in ((out_near, inner), (out_relay, -inner), (out_up, 2), (out_down, -2)):
            out[rows, :] = jnp.where(one == offset, c_one, jnp.where(two == offset, c_two, zero))

    each(surface.shape[1], 256, tiles)
    store.wait()


def sum_body(up, down, relay, out_up, out_down):
    core = lax.axis_index("front") & 1

    @pl.when(core == 0)
    def _():
        out_up[...] = up[...] + relay[...]
        out_down[...] = down[...]

    @pl.when(core == 1)
    def _():
        out_up[...] = up[...]
        out_down[...] = down[...] + relay[...]


def outs_body(first, first_away, second, second_away, third, third_away, out1, out2, out3, t1, t2, t3, sems):
    core = lax.axis_index("front") & 1
    half = first.shape[1]
    rows = block(core, t1.shape[0])
    copies = []
    for i, (own, away, out, total) in enumerate(((first.at[rows, :], first_away.at[rows, :], out1, t1), (second, second_away, out2, t2), (third, third_away, out3, t3))):
        total[:, block(core, half)] = own[...]
        total[:, block(1 - core, half)] = away[...]
        copies.append(pltpu.make_async_copy(total, out, sems.at[i]))
        copies[-1].start()
    for copy in copies:
        copy.wait()


def own_body(surface, v, out):
    def tiles(rows):
        out[rows, :] = mm(surface[0, rows, :], v[...]).astype(BF16)

    each(surface.shape[1], 256, tiles)


def finish_body(part, own, near, back, ahead, *rest):
    out, total, sem = rest[-3:]
    half = own.shape[1]

    def tiles(rows):
        total[rows, :] = (
            own[rows, :].astype(F32) + near[rows, :].astype(F32) + back[rows, :].astype(F32) + ahead[rows, :].astype(F32)
        ).astype(BF16)

    each(own.shape[0], 256, tiles)
    store = pltpu.make_async_copy(total, out.at[:, part * half : (part + 1) * half], sem)
    store.start()
    store.wait()


VMEM = pl.BlockSpec(memory_space=pltpu.VMEM)
SMEM = pl.BlockSpec(memory_space=pltpu.SMEM)
HBM = pl.BlockSpec(memory_space=pltpu.HBM)


def halves(body, args, scalars, extra_outs, scratch, whole, flops):
    shape = jax.ShapeDtypeStruct((args[0].shape[0], 2 * extra_outs[0].shape[1]), BF16) if whole is None else whole
    more = () if whole is None else (whole,)
    return pl.pallas_call(
        body,
        out_shape=[jax.ShapeDtypeStruct(shape.shape, BF16)] + extra_outs[1:],
        in_specs=[VMEM] * len(args) + [SMEM] * len(scalars) + [HBM] * len(more),
        out_specs=[HBM] + [VMEM] * len(extra_outs[1:]),
        scratch_shapes=scratch + [pltpu.SemaphoreType.DMA],
        input_output_aliases={len(args) + len(scalars): 0} if more else {},
        compiler_params=pltpu.CompilerParams(vmem_limit_bytes=12 << 20),
        cost_estimate=pl.CostEstimate(flops=int(flops), bytes_accessed=8 << 20, transcendentals=0),
    )(*args, *scalars, *more)


def stage(args):
    shapes = [args[0].shape, args[1].shape, args[2].shape, (args[0].shape[0],) * 2]
    args = [pltpu.with_memory_space_constraint(a, pltpu.HBM) for a in args]
    return pl.pallas_call(
        stage_body,
        out_shape=[jax.ShapeDtypeStruct(x, BF16) for x in shapes],
        in_specs=[HBM] * len(args),
        out_specs=[VMEM] * 4,
        scratch_shapes=[pltpu.SemaphoreType.DMA((len(args),))],
        compiler_params=pltpu.CompilerParams(vmem_limit_bytes=12 << 20),
        cost_estimate=pl.CostEstimate(flops=0, bytes_accessed=10 << 20, transcendentals=0),
        name="stage",
    )(*args)


def local(
    leaf_load,
    leaf_inverse,
    leaf_coupling,
    leaf_rowmap,
    load_first,
    load_second,
    load_third,
    inverse_first,
    inverse_second,
    inverse_third,
    coupling_first,
    coupling_second,
    rowmap_first,
    rowmap_second,
    surface_coupling,
    neighbor_tiles,
):
    full, panel = leaf_load.shape
    half = panel // 2
    order = leaf_coupling.shape[0]
    square = ((order, order), BF16)
    column = ((order, half), BF16)

    rows = leaf_inverse.shape[0]
    top, low = leaf_inverse[: rows // 2], leaf_inverse[rows // 2 :]
    up_top = shift(top, "col", 1)
    down_low = shift(low, "col", -1)
    up_low = shift(low, "col", 1)
    down_top = shift(top, "col", -1)
    far_top = shift(up_top, "col", 1)
    far_low = shift(down_low, "col", -1)

    n1, n2, n3 = inverse_first.shape[0], inverse_second.shape[0], inverse_third.shape[0]
    pack_x, pack_c, aim = kernel(
        pack_body,
        [((2 * n2 + 2 * n3, order), BF16), ((2 * n1 + n2, order), BF16), ((8, 128), jnp.int32)],
        (rowmap_first, rowmap_second, coupling_first, coupling_second, inverse_first, inverse_second, inverse_third, load_second, load_third),
        fetched=range(9),
        scalars=(neighbor_tiles,),
    )
    pack2 = flip(pack_x, 2)
    pack1 = flip(pack_x, 1)
    away_c = flip(pack_c, 1)
    leaf_c, leaf_ct = kernel(
        leaf_weight_body, [((order, full), BF16), ((full, order), BF16)], (leaf_rowmap, leaf_coupling)
    )
    first_d, first_dt, first_inv, load2 = kernel(
        first_weight_body, [square, square, square, column], (pack_c, away_c, load_second)
    )
    pack3 = flip(pack2, 1)
    second_e, second_et, second_inv, load3, third_near = kernel(
        second_weight_body, [square, square, square, column, ((order // 2, order), BF16)], (pack_x, pack1, pack2, pack3)
    )
    third_far = flip(third_near, 6)

    near_other, near_mine = kernel(
        near_body, [((order, half), F32)] * 2, (leaf_inverse, up_top, down_low, leaf_load, leaf_c, load_first), 2e9
    )
    (other,) = kernel(other_body, [column], (up_low, down_top, far_top, far_low, leaf_load, leaf_c, near_other))
    other = flip(other, 1)
    (mine,) = kernel(mine_body, [((order, half), F32)], (up_low, down_top, far_top, far_low, leaf_load, leaf_c, near_mine))
    rhs_first, term = kernel(first_body, [column] * 2, (mine, other, first_inv, first_d, load2))
    away = flip(term, 2)
    rhs_second, term = kernel(second_body, [column] * 2, (term, away, second_inv, second_e, load3))
    away = flip(term, 6)
    staged = stage((leaf_ct, leaf_load, surface_coupling, leaf_inverse, up_top, up_low, down_top, down_low, far_top, far_low))
    sol_first, second_own, second_away, third_own, third_away = kernel(
        down_body,
        [column, ((n2, half), BF16), ((n2, half), BF16), ((n3, half), BF16), ((n3, half), BF16)],
        (term, away, third_near, third_far, second_et, second_inv, rhs_second, first_dt, first_inv, rhs_first),
        scratch=[pltpu.VMEM(*column)] * 2,
    )
    sol_away = flip(sol_first, 1)

    tail = []
    out_volume = out_tiles = None
    part_shape = jax.ShapeDtypeStruct((full, half), BF16)
    part_scratch = pltpu.VMEM((full, half), BF16)
    for part in range(2):
        out_volume, volume, near, relay, ahead_sum, back_sum = halves(
            functools.partial(volume_body, part),
            (staged[0], staged[1], staged[3], staged[2], sol_first, sol_away, aim),
            (),
            [part_shape] * 6,
            [part_scratch],
            out_volume,
            3e9,
        )
        relay = flip(relay, 1)
        ahead_sum, back_sum = kernel(sum_body, [((full, half), BF16)] * 2, (ahead_sum, back_sum, relay), 1e6)
        from_back = pass_on(ahead_sum, "front", 2)
        from_ahead = pass_on(back_sum, "front", -2)
        near = flip(near, 1)
        (c_own,) = kernel(own_body, [((full, half), BF16)], (staged[2], volume))
        tail.append((c_own, near, from_back, from_ahead))
    for part, terms in enumerate(tail):
        (out_tiles,) = halves(
            functools.partial(finish_body, part), terms, (), [part_shape], [part_scratch], out_tiles, 1e6
        )

    second_away = flip(second_away, 1)
    third_away = flip(third_away, 1)
    shapes = [(n1, panel), (n2, panel), (n3, panel)]
    out_first, out_second, out_third = pl.pallas_call(
        outs_body,
        out_shape=[jax.ShapeDtypeStruct(x, BF16) for x in shapes],
        in_specs=[VMEM] * 6,
        out_specs=[HBM] * 3,
        scratch_shapes=[pltpu.VMEM(x, BF16) for x in shapes] + [pltpu.SemaphoreType.DMA((3,))],
        compiler_params=pltpu.CompilerParams(vmem_limit_bytes=4 << 20),
        cost_estimate=pl.CostEstimate(flops=0, bytes_accessed=1 << 20, transcendentals=0),
        name="outs",
    )(sol_first, sol_away, second_own, second_away, third_own, third_away)
    return (out_volume, out_tiles, out_first, out_second, out_third)


def solution(mesh):
    return jax.shard_map(
        local,
        mesh=mesh,
        in_specs=(
            P("front", "col"),
            P(("front", "col"), None),
            P("front", None),
            P("front", None),
            P("front", "col"),
            P("front", "col"),
            P("front", "col"),
            P("front", None),
            P("front", None),
            P("front", None),
            P(None, "front"),
            P(None, "front"),
            P(),
            P(),
            P("front", None, None),
            P(),
        ),
        out_specs=(P("front", "col"),) * 5,
        check_vma=False,
    )
```

profile of v0, /device:TPU:102, one launch (start us, length us, event | category | flops | bytes accessed | tf_op | source)
XLA Modules:
  0.0 101.2 jit_solution(1507489460136669932)
XLA Ops:
  1.9 1.7 %collective-permute-start = (bf16[128,1024]{1,0:T(8,128)(2,1)S(1)}, bf16[128,1024]{1,0:T(8,128)(2,1)S(1)}, u32[]{:S(2)}, u32[]{:S(2)}) collective-permute-start(bf16[128,1024]{1,0:T(8,128)(2,1)S(1)} %get-tuple-element.102), channel_id=1, source_target_pairs={{0,1},{1,2},{2,3},{3,0},{4,5},{5,6},{6,7},{7,4},{8,9},{9,10},{10,1... | collective-permute-start | bytes 786440 | tf_op jit(solution)/shard_map/ppermute | solution.py:21
  3.5 1.7 %collective-permute-start.3 = (bf16[128,1024]{1,0:T(8,128)(2,1)S(1)}, bf16[128,1024]{1,0:T(8,128)(2,1)S(1)}, u32[]{:S(2)}, u32[]{:S(2)}) collective-permute-start(bf16[128,1024]{1,0:T(8,128)(2,1)S(1)} %get-tuple-element.101), channel_id=1, source_target_pairs={{0,3},{1,0},{2,1},{3,2},{4,7},{5,4},{6,5},{7,6},{8,11},{9,8},{10,9... | collective-permute-start | bytes 786440 | tf_op jit(solution)/shard_map/ppermute | solution.py:21
  6.3 2.8 %shard_map.195 = (bf16[384,512]{1,0:T(8,128)(2,1)S(1)}, bf16[640,512]{1,0:T(8,128)(2,1)S(1)}, s32[8,128]{1,0:T(8,128)S(1)}) custom-call(s32[32,512]{1,0:T(8,128)} %refs_0_.5, s32[16,512]{1,0:T(8,128)} %refs_1_.3, bf16[512,256]{1,0:T(8,128)(2,1)} %refs_2_.2, bf16[512,128]{1,0:T(8,128)(2,1)} %refs_3_.3, bf16[256,512]{1,0:T(8,128)(2,1)} %refs_4_.5, ...), custom_call_target="tpu_custom_call" | custom-call | flops 1000000000 | bytes 1146880 | tf_op jit(solution)/shard_map/pallas_call | solution.py:74
  9.3 2.9 %collective-permute-start.2 = (bf16[128,1024]{1,0:T(8,128)(2,1)S(1)}, bf16[128,1024]{1,0:T(8,128)(2,1)S(1)}, u32[]{:S(2)}, u32[]{:S(2)}) collective-permute-start(bf16[128,1024]{1,0:T(8,128)(2,1)S(1)} %get-tuple-element.102), channel_id=1, source_target_pairs={{0,3},{1,0},{2,1},{3,2},{4,7},{5,4},{6,5},{7,6},{8,11},{9,8},{10,9... | collective-permute-start | bytes 786440 | tf_op jit(solution)/shard_map/ppermute | solution.py:21
  13.5 3.5 %collective-permute-done.1.up_low.refs_0_ = bf16[128,1024]{1,0:T(8,128)(2,1)S(1)} collective-permute-done((bf16[128,1024]{1,0:T(8,128)(2,1)S(1)}, bf16[128,1024]{1,0:T(8,128)(2,1)S(1)}, u32[]{:S(2)}, u32[]{:S(2)}) %collective-permute-start.1) | collective-permute-done | bytes 262176 | tf_op jit(solution)/shard_map/ppermute | solution.py:21
  17.0 2.7 %collective-permute-start.5 = (bf16[128,1024]{1,0:T(8,128)(2,1)S(1)}, bf16[128,1024]{1,0:T(8,128)(2,1)S(1)}, u32[]{:S(2)}, u32[]{:S(2)}) collective-permute-start(bf16[128,1024]{1,0:T(8,128)(2,1)S(1)} %collective-permute-done.3.down_low.refs_2_), channel_id=1, source_target_pairs={{0,3},{1,0},{2,1},{3,2},{4,7},{5,4},{6,5},{7,6},{8,11},{9,8},{10,9... | collective-permute-start | bytes 786440 | tf_op jit(solution)/shard_map/ppermute | solution.py:21
  19.8 1.2 %copy-done.9 = bf16[512,1024]{1,0:T(8,128)(2,1)S(1)} copy-done((bf16[512,1024]{1,0:T(8,128)(2,1)S(1)}, bf16[512,1024]{1,0:T(8,128)(2,1)}, u32[]{:S(2)}) %copy-start.9) | copy-done | bytes 1048600
  21.7 2.2 %shard_map.191 = (bf16[512,1024]{1,0:T(8,128)(2,1)S(1)}, bf16[1024,512]{1,0:T(8,128)(2,1)S(1)}) custom-call(s32[1,512]{1,0:T(1,128)S(1)} %copy-done.12, bf16[512,1024]{1,0:T(8,128)(2,1)S(1)} %copy-done.9), custom_call_target="tpu_custom_call" | custom-call | flops 1000000000 | bytes 1050624 | tf_op jit(solution)/shard_map/pallas_call | solution.py:74
  23.9 1.8 %shard_map.192 = (f32[512,256]{1,0:T(8,128)S(1)}, f32[512,256]{1,0:T(8,128)S(1)}) custom-call(bf16[256,1024]{1,0:T(8,128)(2,1)S(1)} %copy-done.5, bf16[128,1024]{1,0:T(8,128)(2,1)S(1)} %collective-permute-done.up_top.refs_1_, bf16[128,1024]{1,0:T(8,128)(2,1)S(1)} %collective-permute-done.3.down_low.refs_2_, bf16[1024,512]{1,0:T(8,128)(2,1)S(1)} %copy-done, ...), custom_call_target="tpu_custom_call" | custom-call | flops 2000000000 | bytes 3407872 | tf_op jit(solution)/shard_map/pallas_call | solution.py:74
  30.9 1.2 %collective-permute-start.13 = (bf16[256,512]{1,0:T(8,128)(2,1)S(1)}, bf16[256,512]{1,0:T(8,128)(2,1)S(1)}, u32[]{:S(2)}, u32[]{:S(2)}) collective-permute-start(bf16[256,512]{1,0:T(8,128)(2,1)S(1)} %get-tuple-element.71.refs_2_), channel_id=1, source_target_pairs={{0,24},{4,28},{8,16},{12,20},{16,8},{20,12},{24,0},{28,4},{32,56},... | collective-permute-start | bytes 786440 | tf_op jit(solution)/shard_map/ppermute | solution.py:16
  32.1 6.3 %collective-permute-done.8.refs_1_ = bf16[512,256]{1,0:T(8,128)(2,1)S(1)} collective-permute-done((bf16[512,256]{1,0:T(8,128)(2,1)S(1)}, bf16[512,256]{1,0:T(8,128)(2,1)S(1)}, u32[]{:S(2)}, u32[]{:S(2)}) %collective-permute-start.8) | collective-permute-done | bytes 262176 | tf_op jit(solution)/shard_map/ppermute | solution.py:16
  40.5 7.7 %collective-permute-done.12.refs_1_ = bf16[512,256]{1,0:T(8,128)(2,1)S(1)} collective-permute-done((bf16[512,256]{1,0:T(8,128)(2,1)S(1)}, bf16[512,256]{1,0:T(8,128)(2,1)S(1)}, u32[]{:S(2)}, u32[]{:S(2)}) %collective-permute-start.12) | collective-permute-done | bytes 262176 | tf_op jit(solution)/shard_map/ppermute | solution.py:16
  48.2 1.7 %shard_map.200 = (bf16[512,256]{1,0:T(8,128)(2,1)S(1)}, bf16[128,256]{1,0:T(8,128)(2,1)S(1)}, bf16[128,256]{1,0:T(8,128)(2,1)S(1)}, bf16[64,256]{1,0:T(8,128)(2,1)S(1)}, bf16[64,256]{1,0:T(8,128)(2,1)S(1)}) custom-call(bf16[512,256]{1,0:T(8,128)(2,1)S(1)} %get-tuple-element.70.refs_0_, bf16[512,256]{1,0:T(8,128)(2,1)S(1)} %collective-permute-done.12.refs_1_, ...), custom_call_target="tpu_custom_call" | custom-call | flops 1000000000 | bytes 3670016 | tf_op jit(solution)/shard_map/pallas_call | solution.py:74
  50.0 4.2 %stage.1 = (bf16[1024,512]{1,0:T(8,128)(2,1)S(1)}, bf16[1024,512]{1,0:T(8,128)(2,1)S(1)}, bf16[3,1024,1024]{2,1,0:T(8,128)(2,1)S(1)}, bf16[1024,1024]{1,0:T(8,128)(2,1)S(1)}) custom-call(bf16[1024,512]{1,0:T(8,128)(2,1)} %copy-done.6, bf16[1024,512]{1,0:T(8,128)(2,1)} %refs_4_.4, bf16[3,1024,1024]{2,1,0:T(8,128)(2,1)} %surface.1, bf16[256,1024]{1,0:T(8,128)(2,1)} %refs_0_.4, ...), custom_call_target="tpu_custom_call" | custom-call | bytes 10485760 | tf_op jit(solution)/shard_map/stage/pallas_call | solution.py:357
  54.2 4.0 %shard_map.201 = (bf16[1024,512]{1,0:T(8,128)(2,1)}, bf16[1024,256]{1,0:T(8,128)(2,1)S(1)}, bf16[1024,256]{1,0:T(8,128)(2,1)S(1)}, bf16[1024,256]{1,0:T(8,128)(2...) custom-call(bf16[1024,512]{1,0:T(8,128)(2,1)S(1)} %get-tuple-element.54.c_t, ...), custom_call_target="tpu_custom_call" | custom-call | flops 3000000000 | bytes 8388608 | tf_op jit(solution)/shard_map/pallas_call | solution.py:342
  58.8 4.0 %shard_map.202 = (bf16[1024,512]{1,0:T(8,128)(2,1)}, bf16[1024,256]{1,0:T(8,128)(2,1)S(1)}, bf16[1024,256]{1,0:T(8,128)(2,1)S(1)}, bf16[1024,256]{1,0:T(8,128)(2...) custom-call(bf16[1024,512]{1,0:T(8,128)(2,1)S(1)} %get-tuple-element.54.c_t, ...), custom_call_target="tpu_custom_call", output_to_operand_aliasing={{0}: (7, {})} | custom-call | flops 3000000000 | bytes 8388608 | tf_op jit(solution)/shard_map/pallas_call | solution.py:342
  64.8 4.9 %collective-permute-start.21 = (bf16[1024,256]{1,0:T(8,128)(2,1)S(1)}, bf16[1024,256]{1,0:T(8,128)(2,1)S(1)}, u32[]{:S(2)}, u32[]{:S(2)}) collective-permute-start(bf16[1024,256]{1,0:T(8,128)(2,1)S(1)} %get-tuple-element.92), channel_id=1, source_target_pairs={{0,8},{4,12},{8,16},{12,20},{16,24},{20,28},{24,32},{28,36},{32,40... | collective-permute-start | bytes 1572872 | tf_op jit(solution)/shard_map/ppermute | solution.py:26
  69.9 1.9 %collective-permute-start.22 = (bf16[1024,256]{1,0:T(8,128)(2,1)S(1)}, bf16[1024,256]{1,0:T(8,128)(2,1)S(1)}, u32[]{:S(2)}, u32[]{:S(2)}) collective-permute-start(bf16[1024,256]{1,0:T(8,128)(2,1)S(1)} %get-tuple-element.93), channel_id=1, source_target_pairs={{8,0},{12,4},{16,8},{20,12},{24,16},{28,20},{32,24},{36,28},{40,32... | collective-permute-start | bytes 1572872 | tf_op jit(solution)/shard_map/ppermute | solution.py:26
  71.8 7.2 %collective-permute-start.17 = (bf16[1024,256]{1,0:T(8,128)(2,1)S(1)}, bf16[1024,256]{1,0:T(8,128)(2,1)S(1)}, u32[]{:S(2)}, u32[]{:S(2)}) collective-permute-start(bf16[1024,256]{1,0:T(8,128)(2,1)S(1)} %get-tuple-element.85), channel_id=1, source_target_pairs={{0,8},{4,12},{8,16},{12,20},{16,24},{20,28},{24,32},{28,36},{32,40... | collective-permute-start | bytes 1572872 | tf_op jit(solution)/shard_map/ppermute | solution.py:26
  79.1 1.9 %collective-permute-start.18 = (bf16[1024,256]{1,0:T(8,128)(2,1)S(1)}, bf16[1024,256]{1,0:T(8,128)(2,1)S(1)}, u32[]{:S(2)}, u32[]{:S(2)}) collective-permute-start(bf16[1024,256]{1,0:T(8,128)(2,1)S(1)} %get-tuple-element.86), channel_id=1, source_target_pairs={{8,0},{12,4},{16,8},{20,12},{24,16},{28,20},{32,24},{36,28},{40,32... | collective-permute-start | bytes 1572872 | tf_op jit(solution)/shard_map/ppermute | solution.py:26
  81.8 1.2 %shard_map.205.own = bf16[1024,256]{1,0:T(8,128)(2,1)S(1)} custom-call(bf16[3,1024,1024]{2,1,0:T(8,128)(2,1)S(1)} %get-tuple-element.57.surface.refs_0_, bf16[1024,256]{1,0:T(8,128)(2,1)S(1)} %get-tuple-element.87.refs_1_), custom_call_target="tpu_custom_call" | custom-call | flops 1000000000 | bytes 6815744 | tf_op jit(solution)/shard_map/pallas_call | solution.py:74
  84.3 5.6 %collective-permute-done.22.ahead = bf16[1024,256]{1,0:T(8,128)(2,1)S(1)} collective-permute-done((bf16[1024,256]{1,0:T(8,128)(2,1)S(1)}, bf16[1024,256]{1,0:T(8,128)(2,1)S(1)}, u32[]{:S(2)}, u32[]{:S(2)}) %collective-permute-start.22) | collective-permute-done | bytes 524320 | tf_op jit(solution)/shard_map/ppermute | solution.py:26
  91.0 1.5 %collective-permute-done.17.back = bf16[1024,256]{1,0:T(8,128)(2,1)S(1)} collective-permute-done((bf16[1024,256]{1,0:T(8,128)(2,1)S(1)}, bf16[1024,256]{1,0:T(8,128)(2,1)S(1)}, u32[]{:S(2)}, u32[]{:S(2)}) %collective-permute-start.17) | collective-permute-done | bytes 524320 | tf_op jit(solution)/shard_map/ppermute | solution.py:26
  92.4 7.6 %collective-permute-done.18.ahead = bf16[1024,256]{1,0:T(8,128)(2,1)S(1)} collective-permute-done((bf16[1024,256]{1,0:T(8,128)(2,1)S(1)}, bf16[1024,256]{1,0:T(8,128)(2,1)S(1)}, u32[]{:S(2)}, u32[]{:S(2)}) %collective-permute-start.18) | collective-permute-done | bytes 524320 | tf_op jit(solution)/shard_map/ppermute | solution.py:26
  (74 shorter events, 18.6 us)
Async XLA Ops:
  1.9 10.5 %collective-permute-start = (bf16[128,1024]{1,0:T(8,128)(2,1)S(1)}, bf16[128,1024]{1,0:T(8,128)(2,1)S(1)}, u32[]{:S(2)}, u32[]{:S(2)}) collective-permute-start(bf16[128,1024]{1,0:T(8,128)(2,1)S(1)} %get-tuple-element.102), channel_id=1, source_target_pairs={{0,1},{1,2},{2,3},{3,0},{4,5},{5,6},{6,7},{7,4},{8,9},{9,10},{10,1... | collective-permute-start | bytes 786440 | tf_op jit(solution)/shard_map/ppermute | solution.py:21
  3.5 9.6 %collective-permute-start.3 = (bf16[128,1024]{1,0:T(8,128)(2,1)S(1)}, bf16[128,1024]{1,0:T(8,128)(2,1)S(1)}, u32[]{:S(2)}, u32[]{:S(2)}) collective-permute-start(bf16[128,1024]{1,0:T(8,128)(2,1)S(1)} %get-tuple-element.101), channel_id=1, source_target_pairs={{0,3},{1,0},{2,1},{3,2},{4,7},{5,4},{6,5},{7,6},{8,11},{9,8},{10,9... | collective-permute-start | bytes 786440 | tf_op jit(solution)/shard_map/ppermute | solution.py:21
  5.2 11.9 %collective-permute-start.1 = (bf16[128,1024]{1,0:T(8,128)(2,1)S(1)}, bf16[128,1024]{1,0:T(8,128)(2,1)S(1)}, u32[]{:S(2)}, u32[]{:S(2)}) collective-permute-start(bf16[128,1024]{1,0:T(8,128)(2,1)S(1)} %get-tuple-element.101), channel_id=1, source_target_pairs={{0,1},{1,2},{2,3},{3,0},{4,5},{5,6},{6,7},{7,4},{8,9},{9,10},{10,1... | collective-permute-start | bytes 786440 | tf_op jit(solution)/shard_map/ppermute | solution.py:21
  9.2 19.5 %collective-permute-start.7 = (bf16[640,512]{1,0:T(8,128)(2,1)S(1)}, bf16[640,512]{1,0:T(8,128)(2,1)S(1)}, u32[]{:S(2)}, u32[]{:S(2)}) collective-permute-start(bf16[640,512]{1,0:T(8,128)(2,1)S(1)} %get-tuple-element.61.refs_0_), channel_id=1, source_target_pairs={{0,4},{4,0},{8,12},{12,8},{16,20},{20,16},{24,28},{28,24},{32,36},... | collective-permute-start | bytes 1966088 | tf_op jit(solution)/shard_map/ppermute | solution.py:16
  9.3 16.4 %collective-permute-start.2 = (bf16[128,1024]{1,0:T(8,128)(2,1)S(1)}, bf16[128,1024]{1,0:T(8,128)(2,1)S(1)}, u32[]{:S(2)}, u32[]{:S(2)}) collective-permute-start(bf16[128,1024]{1,0:T(8,128)(2,1)S(1)} %get-tuple-element.102), channel_id=1, source_target_pairs={{0,3},{1,0},{2,1},{3,2},{4,7},{5,4},{6,5},{7,6},{8,11},{9,8},{10,9... | collective-permute-start | bytes 786440 | tf_op jit(solution)/shard_map/ppermute | solution.py:21
  12.3 15.1 %collective-permute-start.10 = (bf16[384,512]{1,0:T(8,128)(2,1)S(1)}, bf16[384,512]{1,0:T(8,128)(2,1)S(1)}, u32[]{:S(2)}, u32[]{:S(2)}) collective-permute-start(bf16[384,512]{1,0:T(8,128)(2,1)S(1)} %get-tuple-element.66.refs_0_), channel_id=1, source_target_pairs={{0,8},{4,12},{8,0},{12,4},{16,24},{20,28},{24,16},{28,20},{32,40},... | collective-permute-start | bytes 1179656 | tf_op jit(solution)/shard_map/ppermute | solution.py:16
  13.2 12.5 %collective-permute-start.4 = (bf16[128,1024]{1,0:T(8,128)(2,1)S(1)}, bf16[128,1024]{1,0:T(8,128)(2,1)S(1)}, u32[]{:S(2)}, u32[]{:S(2)}) collective-permute-start(bf16[128,1024]{1,0:T(8,128)(2,1)S(1)} %collective-permute-done.up_top.refs_1_), channel_id=1, source_target_pairs={{0,1},{1,2},{2,3},{3,0},{4,5},{5,6},{6,7},{7,4},{8,9},{9,10},{10,1... | collective-permute-start | bytes 786440 | tf_op jit(solution)/shard_map/ppermute | solution.py:21
  17.0 8.7 %collective-permute-start.5 = (bf16[128,1024]{1,0:T(8,128)(2,1)S(1)}, bf16[128,1024]{1,0:T(8,128)(2,1)S(1)}, u32[]{:S(2)}, u32[]{:S(2)}) collective-permute-start(bf16[128,1024]{1,0:T(8,128)(2,1)S(1)} %collective-permute-done.3.down_low.refs_2_), channel_id=1, source_target_pairs={{0,3},{1,0},{2,1},{3,2},{4,7},{5,4},{6,5},{7,6},{8,11},{9,8},{10,9... | collective-permute-start | bytes 786440 | tf_op jit(solution)/shard_map/ppermute | solution.py:21
  26.8 2.1 %collective-permute-start.6 = (bf16[512,256]{1,0:T(8,128)(2,1)S(1)}, bf16[512,256]{1,0:T(8,128)(2,1)S(1)}, u32[]{:S(2)}, u32[]{:S(2)}) collective-permute-start(bf16[512,256]{1,0:T(8,128)(2,1)S(1)} %shard_map.194), channel_id=1, source_target_pairs={{0,4},{4,0},{8,12},{12,8},{16,20},{20,16},{24,28},{28,24},{32,36},... | collective-permute-start | bytes 786440 | tf_op jit(solution)/shard_map/ppermute | solution.py:16
  26.9 3.7 %collective-permute-start.9 = (bf16[384,512]{1,0:T(8,128)(2,1)S(1)}, bf16[384,512]{1,0:T(8,128)(2,1)S(1)}, u32[]{:S(2)}, u32[]{:S(2)}) collective-permute-start(bf16[384,512]{1,0:T(8,128)(2,1)S(1)} %get-tuple-element.66.refs_0_), channel_id=1, source_target_pairs={{0,4},{4,0},{8,12},{12,8},{16,20},{20,16},{24,28},{28,24},{32,36},... | collective-permute-start | bytes 1179656 | tf_op jit(solution)/shard_map/ppermute | solution.py:16
  27.4 3.2 %collective-permute-start.11 = (bf16[384,512]{1,0:T(8,128)(2,1)S(1)}, bf16[384,512]{1,0:T(8,128)(2,1)S(1)}, u32[]{:S(2)}, u32[]{:S(2)}) collective-permute-start(bf16[384,512]{1,0:T(8,128)(2,1)S(1)} %collective-permute-done.10.refs_2_), channel_id=1, source_target_pairs={{0,4},{4,0},{8,12},{12,8},{16,20},{20,16},{24,28},{28,24},{32,36},... | collective-permute-start | bytes 1179656 | tf_op jit(solution)/shard_map/ppermute | solution.py:16
  29.7 8.7 %collective-permute-start.8 = (bf16[512,256]{1,0:T(8,128)(2,1)S(1)}, bf16[512,256]{1,0:T(8,128)(2,1)S(1)}, u32[]{:S(2)}, u32[]{:S(2)}) collective-permute-start(bf16[512,256]{1,0:T(8,128)(2,1)S(1)} %get-tuple-element.65.refs_0_), channel_id=1, source_target_pairs={{0,8},{4,12},{8,0},{12,4},{16,24},{20,28},{24,16},{28,20},{32,40},... | collective-permute-start | bytes 786440 | tf_op jit(solution)/shard_map/ppermute | solution.py:16
  30.9 9.6 %collective-permute-start.13 = (bf16[256,512]{1,0:T(8,128)(2,1)S(1)}, bf16[256,512]{1,0:T(8,128)(2,1)S(1)}, u32[]{:S(2)}, u32[]{:S(2)}) collective-permute-start(bf16[256,512]{1,0:T(8,128)(2,1)S(1)} %get-tuple-element.71.refs_2_), channel_id=1, source_target_pairs={{0,24},{4,28},{8,16},{12,20},{16,8},{20,12},{24,0},{28,4},{32,56},... | collective-permute-start | bytes 786440 | tf_op jit(solution)/shard_map/ppermute | solution.py:16
  39.2 9.1 %collective-permute-start.12 = (bf16[512,256]{1,0:T(8,128)(2,1)S(1)}, bf16[512,256]{1,0:T(8,128)(2,1)S(1)}, u32[]{:S(2)}, u32[]{:S(2)}) collective-permute-start(bf16[512,256]{1,0:T(8,128)(2,1)S(1)} %get-tuple-element.70.refs_0_), channel_id=1, source_target_pairs={{0,24},{4,28},{8,16},{12,20},{16,8},{20,12},{24,0},{28,4},{32,56},... | collective-permute-start | bytes 786440 | tf_op jit(solution)/shard_map/ppermute | solution.py:16
  49.9 4.3 %collective-permute-start.14 = (bf16[512,256]{1,0:T(8,128)(2,1)S(1)}, bf16[512,256]{1,0:T(8,128)(2,1)S(1)}, u32[]{:S(2)}, u32[]{:S(2)}) collective-permute-start(bf16[512,256]{1,0:T(8,128)(2,1)S(1)} %get-tuple-element.76.s_own.first), channel_id=1, source_target_pairs={{0,4},{4,0},{8,12},{12,8},{16,20},{20,16},{24,28},{28,24},{32,36},... | collective-permute-start | bytes 786440 | tf_op jit(solution)/shard_map/ppermute | solution.py:16
  58.2 5.7 %collective-permute-start.20 = (bf16[1024,256]{1,0:T(8,128)(2,1)S(1)}, bf16[1024,256]{1,0:T(8,128)(2,1)S(1)}, u32[]{:S(2)}, u32[]{:S(2)}) collective-permute-start(bf16[1024,256]{1,0:T(8,128)(2,1)S(1)} %get-tuple-element.91), channel_id=1, source_target_pairs={{0,4},{4,0},{8,12},{12,8},{16,20},{20,16},{24,28},{28,24},{32,36},... | collective-permute-start | bytes 1572872 | tf_op jit(solution)/shard_map/ppermute | solution.py:16
  62.9 16.1 %collective-permute-start.19 = (bf16[1024,256]{1,0:T(8,128)(2,1)S(1)}, bf16[1024,256]{1,0:T(8,128)(2,1)S(1)}, u32[]{:S(2)}, u32[]{:S(2)}) collective-permute-start(bf16[1024,256]{1,0:T(8,128)(2,1)S(1)} %get-tuple-element.88), channel_id=1, source_target_pairs={{0,4},{4,0},{8,12},{12,8},{16,20},{20,16},{24,28},{28,24},{32,36},... | collective-permute-start | bytes 1572872 | tf_op jit(solution)/shard_map/ppermute | solution.py:16
  63.4 8.4 %collective-permute-start.23 = (bf16[128,256]{1,0:T(8,128)(2,1)S(1)}, bf16[128,256]{1,0:T(8,128)(2,1)S(1)}, u32[]{:S(2)}, u32[]{:S(2)}) collective-permute-start(bf16[128,256]{1,0:T(8,128)(2,1)S(1)} %get-tuple-element.95), channel_id=1, source_target_pairs={{0,4},{4,0},{8,12},{12,8},{16,20},{20,16},{24,28},{28,24},{32,36},... | collective-permute-start | bytes 196616 | tf_op jit(solution)/shard_map/ppermute | solution.py:16
  63.5 6.3 %collective-permute-start.24 = (bf16[64,256]{1,0:T(8,128)(2,1)S(1)}, bf16[64,256]{1,0:T(8,128)(2,1)S(1)}, u32[]{:S(2)}, u32[]{:S(2)}) collective-permute-start(bf16[64,256]{1,0:T(8,128)(2,1)S(1)} %get-tuple-element.97), channel_id=1, source_target_pairs={{0,4},{4,0},{8,12},{12,8},{16,20},{20,16},{24,28},{28,24},{32,36},... | collective-permute-start | bytes 98312 | tf_op jit(solution)/shard_map/ppermute | solution.py:16
  63.9 27.0 %collective-permute-start.15 = (bf16[1024,256]{1,0:T(8,128)(2,1)S(1)}, bf16[1024,256]{1,0:T(8,128)(2,1)S(1)}, u32[]{:S(2)}, u32[]{:S(2)}) collective-permute-start(bf16[1024,256]{1,0:T(8,128)(2,1)S(1)} %get-tuple-element.81), channel_id=1, source_target_pairs={{0,4},{4,0},{8,12},{12,8},{16,20},{20,16},{24,28},{28,24},{32,36},... | collective-permute-start | bytes 1572872 | tf_op jit(solution)/shard_map/ppermute | solution.py:16
  64.8 19.5 %collective-permute-start.21 = (bf16[1024,256]{1,0:T(8,128)(2,1)S(1)}, bf16[1024,256]{1,0:T(8,128)(2,1)S(1)}, u32[]{:S(2)}, u32[]{:S(2)}) collective-permute-start(bf16[1024,256]{1,0:T(8,128)(2,1)S(1)} %get-tuple-element.92), channel_id=1, source_target_pairs={{0,8},{4,12},{8,16},{12,20},{16,24},{20,28},{24,32},{28,36},{32,40... | collective-permute-start | bytes 1572872 | tf_op jit(solution)/shard_map/ppermute | solution.py:26
  69.9 20.0 %collective-permute-start.22 = (bf16[1024,256]{1,0:T(8,128)(2,1)S(1)}, bf16[1024,256]{1,0:T(8,128)(2,1)S(1)}, u32[]{:S(2)}, u32[]{:S(2)}) collective-permute-start(bf16[1024,256]{1,0:T(8,128)(2,1)S(1)} %get-tuple-element.93), channel_id=1, source_target_pairs={{8,0},{12,4},{16,8},{20,12},{24,16},{28,20},{32,24},{36,28},{40,32... | collective-permute-start | bytes 1572872 | tf_op jit(solution)/shard_map/ppermute | solution.py:26
  71.8 20.6 %collective-permute-start.17 = (bf16[1024,256]{1,0:T(8,128)(2,1)S(1)}, bf16[1024,256]{1,0:T(8,128)(2,1)S(1)}, u32[]{:S(2)}, u32[]{:S(2)}) collective-permute-start(bf16[1024,256]{1,0:T(8,128)(2,1)S(1)} %get-tuple-element.85), channel_id=1, source_target_pairs={{0,8},{4,12},{8,16},{12,20},{16,24},{20,28},{24,32},{28,36},{32,40... | collective-permute-start | bytes 1572872 | tf_op jit(solution)/shard_map/ppermute | solution.py:26
  79.1 20.9 %collective-permute-start.18 = (bf16[1024,256]{1,0:T(8,128)(2,1)S(1)}, bf16[1024,256]{1,0:T(8,128)(2,1)S(1)}, u32[]{:S(2)}, u32[]{:S(2)}) collective-permute-start(bf16[1024,256]{1,0:T(8,128)(2,1)S(1)} %get-tuple-element.86), channel_id=1, source_target_pairs={{8,0},{12,4},{16,8},{20,12},{24,16},{28,20},{32,24},{36,28},{40,32... | collective-permute-start | bytes 1572872 | tf_op jit(solution)/shard_map/ppermute | solution.py:26
  (14 other events, 133.8 us)
where the time goes:
time: 102 us; the launch traced here: 101 us
  waiting for transfers between devices  33.8 us (33%)
  starting transfers between devices  31.9 us (31%)
  Pallas kernels  30.4 us (30%)
  local copies, waits for them, and re-layouts  3.92 us (4%)
  between operations  1.24 us (1%)
    ppermute x4, starting transfers between devices, pass_on(): lax.ppermute(x, axis, [(i, i + steps) for i in range(count) if 0 <= i + s...  16 us
    ppermute x15, waiting for transfers between devices, flip(): return lax.ppermute(x, 'front', [(i, i ^ mask) for i in range(count)])  15.5 us
    pallas_call x14, Pallas kernels, kernel(): pl.pallas_call(run, out_shape=[jax.ShapeDtypeStruct(s, t) for s, t in out...  15.3 us
    ppermute x4, waiting for transfers between devices, pass_on(): lax.ppermute(x, axis, [(i, i + steps) for i in range(count) if 0 <= i + s...  14.6 us
    pallas_call x4, Pallas kernels, halves(): pl.pallas_call(body, out_shape=[jax.ShapeDtypeStruct(shape.shape, BF16)]...  10.2 us
    ppermute x6, starting transfers between devices, shift(): lax.ppermute(x, axis, [(i, (i + steps) % count) for i in range(count)])  9.71 us
    ppermute x15, starting transfers between devices, flip(): return lax.ppermute(x, 'front', [(i, i ^ mask) for i in range(count)])  6.21 us
    pallas_call x1, Pallas kernels, stage(): pl.pallas_call(stage_body, out_shape=[jax.ShapeDtypeStruct(x, BF16) for x...  4.17 us
  transfers between devices with their start and end apart: 25, of which 9 were waited for; matrix products, arithmetic and copies ran while one was open for 1% of the time, Pallas kernels for 23%

commit v1 on v0

--- a/solution.py
+++ b/solution.py
@@ -21,9 +21,10 @@
     return lax.ppermute(x, axis, [(i, (i + steps) % count) for i in range(count)])
 
 
-def pass_on(x, axis, steps):
-    count = lax.axis_size(axis)
-    return lax.ppermute(x, axis, [(i, i + steps) for i in range(count) if 0 <= i + steps < count])
+def swap_next(x):
+    count = lax.axis_size("front")
+    pairs = [(i, i + 2 if i >> 1 & 1 else i - 2) for i in range(count)]
+    return lax.ppermute(x, "front", [(i, j) for i, j in pairs if 0 <= j < count])
 
 
 def mm(a, b):
@@ -281,18 +282,18 @@
     store.wait()
 
 
-def sum_body(up, down, relay, out_up, out_down):
-    core = lax.axis_index("front") & 1
-
-    @pl.when(core == 0)
-    def _():
-        out_up[...] = up[...] + relay[...]
-        out_down[...] = down[...]
-
-    @pl.when(core == 1)
-    def _():
-        out_up[...] = up[...]
-        out_down[...] = down[...] + relay[...]
+def sum_body(up, down, relay, out_inner, out_outer):
+    front = lax.axis_index("front")
+    core = front & 1
+    even = (front >> 1) & 1 == 0
+    for which in (0, 1):
+        for parity in (True, False):
+
+            @pl.when((core == which) & (even == parity))
+            def _():
+                to_up, to_down = (out_inner, out_outer) if parity else (out_outer, out_inner)
+                to_up[...] = up[...] + relay[...] if which == 0 else up[...]
+                to_down[...] = down[...] + relay[...] if which == 1 else down[...]
 
 
 def outs_body(first, first_away, second, second_away, third, third_away, out1, out2, out3, t1, t2, t3, sems):
@@ -456,12 +457,12 @@
             3e9,
         )
         relay = flip(relay, 1)
-        ahead_sum, back_sum = kernel(sum_body, [((full, half), BF16)] * 2, (ahead_sum, back_sum, relay), 1e6)
-        from_back = pass_on(ahead_sum, "front", 2)
-        from_ahead = pass_on(back_sum, "front", -2)
+        inner, outer = kernel(sum_body, [((full, half), BF16)] * 2, (ahead_sum, back_sum, relay), 1e6)
+        from_outer = swap_next(outer)
+        from_inner = flip(inner, 2)
         near = flip(near, 1)
         (c_own,) = kernel(own_body, [((full, half), BF16)], (staged[2], volume))
-        tail.append((c_own, near, from_back, from_ahead))
+        tail.append((c_own, near, from_outer, from_inner))
     for part, terms in enumerate(tail):
         (out_tiles,) = halves(
             functools.partial(finish_body, part), terms, (), [part_shape], [part_scratch], out_tiles, 1e6

time: 102 us -> 96.7 us (0.948)
  the two profiles are of different devices: /device:TPU:102 before, /device:TPU:129 now
where the time goes in v1:
time: 96.7 us; the launch traced here: 95.9 us
  starting transfers between devices  31.3 us (32%)
  Pallas kernels  30.4 us (31%)
  waiting for transfers between devices  29 us (30%)
  local copies, waits for them, and re-layouts  3.92 us (4%)
  between operations  1.21 us (1%)
    ppermute x2, waiting for transfers between devices, swap_next(): lax.ppermute(x, 'front', [(i, j) for i, j in pairs if 0 <= j < count])  16.2 us
    ppermute x17, starting transfers between devices, flip(): return lax.ppermute(x, 'front', [(i, i ^ mask) for i in range(count)])  15.8 us
    pallas_call x14, Pallas kernels, kernel(): pl.pallas_call(run, out_shape=[jax.ShapeDtypeStruct(s, t) for s, t in out...  15.3 us
    ppermute x17, waiting for transfers between devices, flip(): return lax.ppermute(x, 'front', [(i, i ^ mask) for i in range(count)])  10.5 us
    pallas_call x4, Pallas kernels, halves(): pl.pallas_call(body, out_shape=[jax.ShapeDtypeStruct(shape.shape, BF16)]...  10.2 us
    ppermute x2, starting transfers between devices, swap_next(): lax.ppermute(x, 'front', [(i, j) for i, j in pairs if 0 <= j < count])  8.59 us
    ppermute x6, starting transfers between devices, shift(): lax.ppermute(x, axis, [(i, (i + steps) % count) for i in range(count)])  6.9 us
    pallas_call x1, Pallas kernels, stage(): pl.pallas_call(stage_body, out_shape=[jax.ShapeDtypeStruct(x, BF16) for x...  4.15 us
  transfers between devices with their start and end apart: 25, of which 6 were waited for; matrix products, arithmetic and copies ran while one was open for 1% of the time, Pallas kernels for 25%

profile of v1, /device:TPU:129, one launch (start us, length us, event | category | flops | bytes accessed | tf_op | source)
XLA Modules:
  0.0 95.9 jit_solution(9407005055150964825)
XLA Ops:
  1.9 1.4 %collective-permute-start = (bf16[128,1024]{1,0:T(8,128)(2,1)S(1)}, bf16[128,1024]{1,0:T(8,128)(2,1)S(1)}, u32[]{:S(2)}, u32[]{:S(2)}) collective-permute-start(bf16[128,1024]{1,0:T(8,128)(2,1)S(1)} %get-tuple-element.102), channel_id=1, source_target_pairs={{0,1},{1,2},{2,3},{3,0},{4,5},{5,6},{6,7},{7,4},{8,9},{9,10},{10,1... | collective-permute-start | bytes 786440 | tf_op jit(solution)/shard_map/ppermute | solution.py:21
  3.2 1.5 %collective-permute-start.3 = (bf16[128,1024]{1,0:T(8,128)(2,1)S(1)}, bf16[128,1024]{1,0:T(8,128)(2,1)S(1)}, u32[]{:S(2)}, u32[]{:S(2)}) collective-permute-start(bf16[128,1024]{1,0:T(8,128)(2,1)S(1)} %get-tuple-element.101), channel_id=1, source_target_pairs={{0,3},{1,0},{2,1},{3,2},{4,7},{5,4},{6,5},{7,6},{8,11},{9,8},{10,9... | collective-permute-start | bytes 786440 | tf_op jit(solution)/shard_map/ppermute | solution.py:21
  5.5 2.8 %shard_map.195 = (bf16[384,512]{1,0:T(8,128)(2,1)S(1)}, bf16[640,512]{1,0:T(8,128)(2,1)S(1)}, s32[8,128]{1,0:T(8,128)S(1)}) custom-call(s32[32,512]{1,0:T(8,128)} %refs_0_.5, s32[16,512]{1,0:T(8,128)} %refs_1_.3, bf16[512,256]{1,0:T(8,128)(2,1)} %refs_2_.2, bf16[512,128]{1,0:T(8,128)(2,1)} %refs_3_.3, bf16[256,512]{1,0:T(8,128)(2,1)} %refs_4_.5, ...), custom_call_target="tpu_custom_call" | custom-call | flops 1000000000 | bytes 1146880 | tf_op jit(solution)/shard_map/pallas_call | solution.py:75
  8.4 1.5 %collective-permute-start.7 = (bf16[640,512]{1,0:T(8,128)(2,1)S(1)}, bf16[640,512]{1,0:T(8,128)(2,1)S(1)}, u32[]{:S(2)}, u32[]{:S(2)}) collective-permute-start(bf16[640,512]{1,0:T(8,128)(2,1)S(1)} %get-tuple-element.61.refs_0_), channel_id=1, source_target_pairs={{0,4},{4,0},{8,12},{12,8},{16,20},{20,16},{24,28},{28,24},{32,36},... | collective-permute-start | bytes 1966088 | tf_op jit(solution)/shard_map/ppermute | solution.py:16
  9.9 2.6 %collective-permute-start.2 = (bf16[128,1024]{1,0:T(8,128)(2,1)S(1)}, bf16[128,1024]{1,0:T(8,128)(2,1)S(1)}, u32[]{:S(2)}, u32[]{:S(2)}) collective-permute-start(bf16[128,1024]{1,0:T(8,128)(2,1)S(1)} %get-tuple-element.102), channel_id=1, source_target_pairs={{0,3},{1,0},{2,1},{3,2},{4,7},{5,4},{6,5},{7,6},{8,11},{9,8},{10,9... | collective-permute-start | bytes 786440 | tf_op jit(solution)/shard_map/ppermute | solution.py:21
  13.7 2.3 %collective-permute-done.1.up_low.refs_0_ = bf16[128,1024]{1,0:T(8,128)(2,1)S(1)} collective-permute-done((bf16[128,1024]{1,0:T(8,128)(2,1)S(1)}, bf16[128,1024]{1,0:T(8,128)(2,1)S(1)}, u32[]{:S(2)}, u32[]{:S(2)}) %collective-permute-start.1) | collective-permute-done | bytes 262176 | tf_op jit(solution)/shard_map/ppermute | solution.py:21
  16.1 1.4 %collective-permute-start.5 = (bf16[128,1024]{1,0:T(8,128)(2,1)S(1)}, bf16[128,1024]{1,0:T(8,128)(2,1)S(1)}, u32[]{:S(2)}, u32[]{:S(2)}) collective-permute-start(bf16[128,1024]{1,0:T(8,128)(2,1)S(1)} %collective-permute-done.3.down_low.refs_2_), channel_id=1, source_target_pairs={{0,3},{1,0},{2,1},{3,2},{4,7},{5,4},{6,5},{7,6},{8,11},{9,8},{10,9... | collective-permute-start | bytes 786440 | tf_op jit(solution)/shard_map/ppermute | solution.py:21
  19.4 2.2 %shard_map.191 = (bf16[512,1024]{1,0:T(8,128)(2,1)S(1)}, bf16[1024,512]{1,0:T(8,128)(2,1)S(1)}) custom-call(s32[1,512]{1,0:T(1,128)S(1)} %copy-done.12, bf16[512,1024]{1,0:T(8,128)(2,1)S(1)} %copy-done.9), custom_call_target="tpu_custom_call" | custom-call | flops 1000000000 | bytes 1050624 | tf_op jit(solution)/shard_map/pallas_call | solution.py:75
  21.6 1.8 %shard_map.192 = (f32[512,256]{1,0:T(8,128)S(1)}, f32[512,256]{1,0:T(8,128)S(1)}) custom-call(bf16[256,1024]{1,0:T(8,128)(2,1)S(1)} %copy-done.5, bf16[128,1024]{1,0:T(8,128)(2,1)S(1)} %collective-permute-done.up_top.refs_1_, bf16[128,1024]{1,0:T(8,128)(2,1)S(1)} %collective-permute-done.3.down_low.refs_2_, bf16[1024,512]{1,0:T(8,128)(2,1)S(1)} %copy-done, ...), custom_call_target="tpu_custom_call" | custom-call | flops 2000000000 | bytes 3407872 | tf_op jit(solution)/shard_map/pallas_call | solution.py:75
  24.6 3.0 %collective-permute-start.6 = (bf16[512,256]{1,0:T(8,128)(2,1)S(1)}, bf16[512,256]{1,0:T(8,128)(2,1)S(1)}, u32[]{:S(2)}, u32[]{:S(2)}) collective-permute-start(bf16[512,256]{1,0:T(8,128)(2,1)S(1)} %shard_map.194), channel_id=1, source_target_pairs={{0,4},{4,0},{8,12},{12,8},{16,20},{20,16},{24,28},{28,24},{32,36},... | collective-permute-start | bytes 786440 | tf_op jit(solution)/shard_map/ppermute | solution.py:16
  30.3 1.3 %collective-permute-start.8 = (bf16[512,256]{1,0:T(8,128)(2,1)S(1)}, bf16[512,256]{1,0:T(8,128)(2,1)S(1)}, u32[]{:S(2)}, u32[]{:S(2)}) collective-permute-start(bf16[512,256]{1,0:T(8,128)(2,1)S(1)} %get-tuple-element.65.refs_0_), channel_id=1, source_target_pairs={{0,8},{4,12},{8,0},{12,4},{16,24},{20,28},{24,16},{28,20},{32,40},... | collective-permute-start | bytes 786440 | tf_op jit(solution)/shard_map/ppermute | solution.py:16
  31.9 1.9 %collective-permute-start.13 = (bf16[256,512]{1,0:T(8,128)(2,1)S(1)}, bf16[256,512]{1,0:T(8,128)(2,1)S(1)}, u32[]{:S(2)}, u32[]{:S(2)}) collective-permute-start(bf16[256,512]{1,0:T(8,128)(2,1)S(1)} %get-tuple-element.71.refs_2_), channel_id=1, source_target_pairs={{0,24},{4,28},{8,16},{12,20},{16,8},{20,12},{24,0},{28,4},{32,56},... | collective-permute-start | bytes 786440 | tf_op jit(solution)/shard_map/ppermute | solution.py:16
  33.8 4.4 %collective-permute-done.8.refs_1_ = bf16[512,256]{1,0:T(8,128)(2,1)S(1)} collective-permute-done((bf16[512,256]{1,0:T(8,128)(2,1)S(1)}, bf16[512,256]{1,0:T(8,128)(2,1)S(1)}, u32[]{:S(2)}, u32[]{:S(2)}) %collective-permute-start.8) | collective-permute-done | bytes 262176 | tf_op jit(solution)/shard_map/ppermute | solution.py:16
  38.9 2.6 %collective-permute-start.12 = (bf16[512,256]{1,0:T(8,128)(2,1)S(1)}, bf16[512,256]{1,0:T(8,128)(2,1)S(1)}, u32[]{:S(2)}, u32[]{:S(2)}) collective-permute-start(bf16[512,256]{1,0:T(8,128)(2,1)S(1)} %get-tuple-element.70.refs_0_), channel_id=1, source_target_pairs={{0,24},{4,28},{8,16},{12,20},{16,8},{20,12},{24,0},{28,4},{32,56},... | collective-permute-start | bytes 786440 | tf_op jit(solution)/shard_map/ppermute | solution.py:16
  41.5 5.6 %collective-permute-done.12.refs_1_ = bf16[512,256]{1,0:T(8,128)(2,1)S(1)} collective-permute-done((bf16[512,256]{1,0:T(8,128)(2,1)S(1)}, bf16[512,256]{1,0:T(8,128)(2,1)S(1)}, u32[]{:S(2)}, u32[]{:S(2)}) %collective-permute-start.12) | collective-permute-done | bytes 262176 | tf_op jit(solution)/shard_map/ppermute | solution.py:16
  47.1 1.7 %shard_map.200 = (bf16[512,256]{1,0:T(8,128)(2,1)S(1)}, bf16[128,256]{1,0:T(8,128)(2,1)S(1)}, bf16[128,256]{1,0:T(8,128)(2,1)S(1)}, bf16[64,256]{1,0:T(8,128)(2,1)S(1)}, bf16[64,256]{1,0:T(8,128)(2,1)S(1)}) custom-call(bf16[512,256]{1,0:T(8,128)(2,1)S(1)} %get-tuple-element.70.refs_0_, bf16[512,256]{1,0:T(8,128)(2,1)S(1)} %collective-permute-done.12.refs_1_, ...), custom_call_target="tpu_custom_call" | custom-call | flops 1000000000 | bytes 3670016 | tf_op jit(solution)/shard_map/pallas_call | solution.py:75
  48.8 1.9 %collective-permute-start.14 = (bf16[512,256]{1,0:T(8,128)(2,1)S(1)}, bf16[512,256]{1,0:T(8,128)(2,1)S(1)}, u32[]{:S(2)}, u32[]{:S(2)}) collective-permute-start(bf16[512,256]{1,0:T(8,128)(2,1)S(1)} %get-tuple-element.76.s_own.first), channel_id=1, source_target_pairs={{0,4},{4,0},{8,12},{12,8},{16,20},{20,16},{24,28},{28,24},{32,36},... | collective-permute-start | bytes 786440 | tf_op jit(solution)/shard_map/ppermute | solution.py:16
  50.7 4.2 %stage.1 = (bf16[1024,512]{1,0:T(8,128)(2,1)S(1)}, bf16[1024,512]{1,0:T(8,128)(2,1)S(1)}, bf16[3,1024,1024]{2,1,0:T(8,128)(2,1)S(1)}, bf16[1024,1024]{1,0:T(8,128)(2,1)S(1)}) custom-call(bf16[1024,512]{1,0:T(8,128)(2,1)} %copy-done.6, bf16[1024,512]{1,0:T(8,128)(2,1)} %refs_4_.4, bf16[3,1024,1024]{2,1,0:T(8,128)(2,1)} %surface.1, bf16[256,1024]{1,0:T(8,128)(2,1)} %refs_0_.4, ...), custom_call_target="tpu_custom_call" | custom-call | bytes 10485760 | tf_op jit(solution)/shard_map/stage/pallas_call | solution.py:358
  54.9 4.0 %shard_map.201 = (bf16[1024,512]{1,0:T(8,128)(2,1)}, bf16[1024,256]{1,0:T(8,128)(2,1)S(1)}, bf16[1024,256]{1,0:T(8,128)(2,1)S(1)}, bf16[1024,256]{1,0:T(8,128)(2...) custom-call(bf16[1024,512]{1,0:T(8,128)(2,1)S(1)} %get-tuple-element.54.c_t, ...), custom_call_target="tpu_custom_call" | custom-call | flops 3000000000 | bytes 8388608 | tf_op jit(solution)/shard_map/pallas_call | solution.py:343
  59.0 4.0 %shard_map.202 = (bf16[1024,512]{1,0:T(8,128)(2,1)}, bf16[1024,256]{1,0:T(8,128)(2,1)S(1)}, bf16[1024,256]{1,0:T(8,128)(2,1)S(1)}, bf16[1024,256]{1,0:T(8,128)(2...) custom-call(bf16[1024,512]{1,0:T(8,128)(2,1)S(1)} %get-tuple-element.54.c_t, ...), custom_call_target="tpu_custom_call", output_to_operand_aliasing={{0}: (7, {})} | custom-call | flops 3000000000 | bytes 8388608 | tf_op jit(solution)/shard_map/pallas_call | solution.py:343
  65.1 4.0 %collective-permute-start.21 = (bf16[1024,256]{1,0:T(8,128)(2,1)S(1)}, bf16[1024,256]{1,0:T(8,128)(2,1)S(1)}, u32[]{:S(2)}, u32[]{:S(2)}) collective-permute-start(bf16[1024,256]{1,0:T(8,128)(2,1)S(1)} %get-tuple-element.92), channel_id=1, source_target_pairs={{8,16},{12,20},{16,8},{20,12},{24,32},{28,36},{32,24},{36,28},{40,... | collective-permute-start | bytes 1572872 | tf_op jit(solution)/shard_map/ppermute | solution.py:27
  69.3 4.6 %collective-permute-start.17 = (bf16[1024,256]{1,0:T(8,128)(2,1)S(1)}, bf16[1024,256]{1,0:T(8,128)(2,1)S(1)}, u32[]{:S(2)}, u32[]{:S(2)}) collective-permute-start(bf16[1024,256]{1,0:T(8,128)(2,1)S(1)} %get-tuple-element.85), channel_id=1, source_target_pairs={{8,16},{12,20},{16,8},{20,12},{24,32},{28,36},{32,24},{36,28},{40,... | collective-permute-start | bytes 1572872 | tf_op jit(solution)/shard_map/ppermute | solution.py:27
  77.3 6.1 %collective-permute-done.21.back = bf16[1024,256]{1,0:T(8,128)(2,1)S(1)} collective-permute-done((bf16[1024,256]{1,0:T(8,128)(2,1)S(1)}, bf16[1024,256]{1,0:T(8,128)(2,1)S(1)}, u32[]{:S(2)}, u32[]{:S(2)}) %collective-permute-start.21) | collective-permute-done | bytes 524320 | tf_op jit(solution)/shard_map/ppermute | solution.py:27
  84.5 10.1 %collective-permute-done.17.back = bf16[1024,256]{1,0:T(8,128)(2,1)S(1)} collective-permute-done((bf16[1024,256]{1,0:T(8,128)(2,1)S(1)}, bf16[1024,256]{1,0:T(8,128)(2,1)S(1)}, u32[]{:S(2)}, u32[]{:S(2)}) %collective-permute-start.17) | collective-permute-done | bytes 524320 | tf_op jit(solution)/shard_map/ppermute | solution.py:27
  (74 shorter events, 17.7 us)
Async XLA Ops:
  1.9 10.7 %collective-permute-start = (bf16[128,1024]{1,0:T(8,128)(2,1)S(1)}, bf16[128,1024]{1,0:T(8,128)(2,1)S(1)}, u32[]{:S(2)}, u32[]{:S(2)}) collective-permute-start(bf16[128,1024]{1,0:T(8,128)(2,1)S(1)} %get-tuple-element.102), channel_id=1, source_target_pairs={{0,1},{1,2},{2,3},{3,0},{4,5},{5,6},{6,7},{7,4},{8,9},{9,10},{10,1... | collective-permute-start | bytes 786440 | tf_op jit(solution)/shard_map/ppermute | solution.py:21
  3.2 10.5 %collective-permute-start.3 = (bf16[128,1024]{1,0:T(8,128)(2,1)S(1)}, bf16[128,1024]{1,0:T(8,128)(2,1)S(1)}, u32[]{:S(2)}, u32[]{:S(2)}) collective-permute-start(bf16[128,1024]{1,0:T(8,128)(2,1)S(1)} %get-tuple-element.101), channel_id=1, source_target_pairs={{0,3},{1,0},{2,1},{3,2},{4,7},{5,4},{6,5},{7,6},{8,11},{9,8},{10,9... | collective-permute-start | bytes 786440 | tf_op jit(solution)/shard_map/ppermute | solution.py:21
  4.8 11.3 %collective-permute-start.1 = (bf16[128,1024]{1,0:T(8,128)(2,1)S(1)}, bf16[128,1024]{1,0:T(8,128)(2,1)S(1)}, u32[]{:S(2)}, u32[]{:S(2)}) collective-permute-start(bf16[128,1024]{1,0:T(8,128)(2,1)S(1)} %get-tuple-element.101), channel_id=1, source_target_pairs={{0,1},{1,2},{2,3},{3,0},{4,5},{5,6},{6,7},{7,4},{8,9},{9,10},{10,1... | collective-permute-start | bytes 786440 | tf_op jit(solution)/shard_map/ppermute | solution.py:21
  8.4 20.8 %collective-permute-start.7 = (bf16[640,512]{1,0:T(8,128)(2,1)S(1)}, bf16[640,512]{1,0:T(8,128)(2,1)S(1)}, u32[]{:S(2)}, u32[]{:S(2)}) collective-permute-start(bf16[640,512]{1,0:T(8,128)(2,1)S(1)} %get-tuple-element.61.refs_0_), channel_id=1, source_target_pairs={{0,4},{4,0},{8,12},{12,8},{16,20},{20,16},{24,28},{28,24},{32,36},... | collective-permute-start | bytes 1966088 | tf_op jit(solution)/shard_map/ppermute | solution.py:16
  9.9 13.5 %collective-permute-start.2 = (bf16[128,1024]{1,0:T(8,128)(2,1)S(1)}, bf16[128,1024]{1,0:T(8,128)(2,1)S(1)}, u32[]{:S(2)}, u32[]{:S(2)}) collective-permute-start(bf16[128,1024]{1,0:T(8,128)(2,1)S(1)} %get-tuple-element.102), channel_id=1, source_target_pairs={{0,3},{1,0},{2,1},{3,2},{4,7},{5,4},{6,5},{7,6},{8,11},{9,8},{10,9... | collective-permute-start | bytes 786440 | tf_op jit(solution)/shard_map/ppermute | solution.py:21
  12.5 15.2 %collective-permute-start.10 = (bf16[384,512]{1,0:T(8,128)(2,1)S(1)}, bf16[384,512]{1,0:T(8,128)(2,1)S(1)}, u32[]{:S(2)}, u32[]{:S(2)}) collective-permute-start(bf16[384,512]{1,0:T(8,128)(2,1)S(1)} %get-tuple-element.66.refs_0_), channel_id=1, source_target_pairs={{0,8},{4,12},{8,0},{12,4},{16,24},{20,28},{24,16},{28,20},{32,40},... | collective-permute-start | bytes 1179656 | tf_op jit(solution)/shard_map/ppermute | solution.py:16
  13.7 9.7 %collective-permute-start.4 = (bf16[128,1024]{1,0:T(8,128)(2,1)S(1)}, bf16[128,1024]{1,0:T(8,128)(2,1)S(1)}, u32[]{:S(2)}, u32[]{:S(2)}) collective-permute-start(bf16[128,1024]{1,0:T(8,128)(2,1)S(1)} %collective-permute-done.up_top.refs_1_), channel_id=1, source_target_pairs={{0,1},{1,2},{2,3},{3,0},{4,5},{5,6},{6,7},{7,4},{8,9},{9,10},{10,1... | collective-permute-start | bytes 786440 | tf_op jit(solution)/shard_map/ppermute | solution.py:21
  16.1 7.4 %collective-permute-start.5 = (bf16[128,1024]{1,0:T(8,128)(2,1)S(1)}, bf16[128,1024]{1,0:T(8,128)(2,1)S(1)}, u32[]{:S(2)}, u32[]{:S(2)}) collective-permute-start(bf16[128,1024]{1,0:T(8,128)(2,1)S(1)} %collective-permute-done.3.down_low.refs_2_), channel_id=1, source_target_pairs={{0,3},{1,0},{2,1},{3,2},{4,7},{5,4},{6,5},{7,6},{8,11},{9,8},{10,9... | collective-permute-start | bytes 786440 | tf_op jit(solution)/shard_map/ppermute | solution.py:21
  24.6 4.9 %collective-permute-start.6 = (bf16[512,256]{1,0:T(8,128)(2,1)S(1)}, bf16[512,256]{1,0:T(8,128)(2,1)S(1)}, u32[]{:S(2)}, u32[]{:S(2)}) collective-permute-start(bf16[512,256]{1,0:T(8,128)(2,1)S(1)} %shard_map.194), channel_id=1, source_target_pairs={{0,4},{4,0},{8,12},{12,8},{16,20},{20,16},{24,28},{28,24},{32,36},... | collective-permute-start | bytes 786440 | tf_op jit(solution)/shard_map/ppermute | solution.py:16
  27.6 4.0 %collective-permute-start.9 = (bf16[384,512]{1,0:T(8,128)(2,1)S(1)}, bf16[384,512]{1,0:T(8,128)(2,1)S(1)}, u32[]{:S(2)}, u32[]{:S(2)}) collective-permute-start(bf16[384,512]{1,0:T(8,128)(2,1)S(1)} %get-tuple-element.66.refs_0_), channel_id=1, source_target_pairs={{0,4},{4,0},{8,12},{12,8},{16,20},{20,16},{24,28},{28,24},{32,36},... | collective-permute-start | bytes 1179656 | tf_op jit(solution)/shard_map/ppermute | solution.py:16
  27.7 3.9 %collective-permute-start.11 = (bf16[384,512]{1,0:T(8,128)(2,1)S(1)}, bf16[384,512]{1,0:T(8,128)(2,1)S(1)}, u32[]{:S(2)}, u32[]{:S(2)}) collective-permute-start(bf16[384,512]{1,0:T(8,128)(2,1)S(1)} %collective-permute-done.10.refs_2_), channel_id=1, source_target_pairs={{0,4},{4,0},{8,12},{12,8},{16,20},{20,16},{24,28},{28,24},{32,36},... | collective-permute-start | bytes 1179656 | tf_op jit(solution)/shard_map/ppermute | solution.py:16
  30.3 7.9 %collective-permute-start.8 = (bf16[512,256]{1,0:T(8,128)(2,1)S(1)}, bf16[512,256]{1,0:T(8,128)(2,1)S(1)}, u32[]{:S(2)}, u32[]{:S(2)}) collective-permute-start(bf16[512,256]{1,0:T(8,128)(2,1)S(1)} %get-tuple-element.65.refs_0_), channel_id=1, source_target_pairs={{0,8},{4,12},{8,0},{12,4},{16,24},{20,28},{24,16},{28,20},{32,40},... | collective-permute-start | bytes 786440 | tf_op jit(solution)/shard_map/ppermute | solution.py:16
  31.9 9.6 %collective-permute-start.13 = (bf16[256,512]{1,0:T(8,128)(2,1)S(1)}, bf16[256,512]{1,0:T(8,128)(2,1)S(1)}, u32[]{:S(2)}, u32[]{:S(2)}) collective-permute-start(bf16[256,512]{1,0:T(8,128)(2,1)S(1)} %get-tuple-element.71.refs_2_), channel_id=1, source_target_pairs={{0,24},{4,28},{8,16},{12,20},{16,8},{20,12},{24,0},{28,4},{32,56},... | collective-permute-start | bytes 786440 | tf_op jit(solution)/shard_map/ppermute | solution.py:16
  38.9 8.2 %collective-permute-start.12 = (bf16[512,256]{1,0:T(8,128)(2,1)S(1)}, bf16[512,256]{1,0:T(8,128)(2,1)S(1)}, u32[]{:S(2)}, u32[]{:S(2)}) collective-permute-start(bf16[512,256]{1,0:T(8,128)(2,1)S(1)} %get-tuple-element.70.refs_0_), channel_id=1, source_target_pairs={{0,24},{4,28},{8,16},{12,20},{16,8},{20,12},{24,0},{28,4},{32,56},... | collective-permute-start | bytes 786440 | tf_op jit(solution)/shard_map/ppermute | solution.py:16
  48.8 6.1 %collective-permute-start.14 = (bf16[512,256]{1,0:T(8,128)(2,1)S(1)}, bf16[512,256]{1,0:T(8,128)(2,1)S(1)}, u32[]{:S(2)}, u32[]{:S(2)}) collective-permute-start(bf16[512,256]{1,0:T(8,128)(2,1)S(1)} %get-tuple-element.76.s_own.first), channel_id=1, source_target_pairs={{0,4},{4,0},{8,12},{12,8},{16,20},{20,16},{24,28},{28,24},{32,36},... | collective-permute-start | bytes 786440 | tf_op jit(solution)/shard_map/ppermute | solution.py:16
  58.9 5.3 %collective-permute-start.20 = (bf16[1024,256]{1,0:T(8,128)(2,1)S(1)}, bf16[1024,256]{1,0:T(8,128)(2,1)S(1)}, u32[]{:S(2)}, u32[]{:S(2)}) collective-permute-start(bf16[1024,256]{1,0:T(8,128)(2,1)S(1)} %get-tuple-element.91), channel_id=1, source_target_pairs={{0,4},{4,0},{8,12},{12,8},{16,20},{20,16},{24,28},{28,24},{32,36},... | collective-permute-start | bytes 1572872 | tf_op jit(solution)/shard_map/ppermute | solution.py:16
  63.6 10.4 %collective-permute-start.19 = (bf16[1024,256]{1,0:T(8,128)(2,1)S(1)}, bf16[1024,256]{1,0:T(8,128)(2,1)S(1)}, u32[]{:S(2)}, u32[]{:S(2)}) collective-permute-start(bf16[1024,256]{1,0:T(8,128)(2,1)S(1)} %get-tuple-element.88), channel_id=1, source_target_pairs={{0,4},{4,0},{8,12},{12,8},{16,20},{20,16},{24,28},{28,24},{32,36},... | collective-permute-start | bytes 1572872 | tf_op jit(solution)/shard_map/ppermute | solution.py:16
  63.7 5.6 %collective-permute-start.23 = (bf16[128,256]{1,0:T(8,128)(2,1)S(1)}, bf16[128,256]{1,0:T(8,128)(2,1)S(1)}, u32[]{:S(2)}, u32[]{:S(2)}) collective-permute-start(bf16[128,256]{1,0:T(8,128)(2,1)S(1)} %get-tuple-element.95), channel_id=1, source_target_pairs={{0,4},{4,0},{8,12},{12,8},{16,20},{20,16},{24,28},{28,24},{32,36},... | collective-permute-start | bytes 196616 | tf_op jit(solution)/shard_map/ppermute | solution.py:16
  64.1 5.1 %collective-permute-start.24 = (bf16[64,256]{1,0:T(8,128)(2,1)S(1)}, bf16[64,256]{1,0:T(8,128)(2,1)S(1)}, u32[]{:S(2)}, u32[]{:S(2)}) collective-permute-start(bf16[64,256]{1,0:T(8,128)(2,1)S(1)} %get-tuple-element.97), channel_id=1, source_target_pairs={{0,4},{4,0},{8,12},{12,8},{16,20},{20,16},{24,28},{28,24},{32,36},... | collective-permute-start | bytes 98312 | tf_op jit(solution)/shard_map/ppermute | solution.py:16
  64.2 20.3 %collective-permute-start.15 = (bf16[1024,256]{1,0:T(8,128)(2,1)S(1)}, bf16[1024,256]{1,0:T(8,128)(2,1)S(1)}, u32[]{:S(2)}, u32[]{:S(2)}) collective-permute-start(bf16[1024,256]{1,0:T(8,128)(2,1)S(1)} %get-tuple-element.81), channel_id=1, source_target_pairs={{0,4},{4,0},{8,12},{12,8},{16,20},{20,16},{24,28},{28,24},{32,36},... | collective-permute-start | bytes 1572872 | tf_op jit(solution)/shard_map/ppermute | solution.py:16
  65.1 18.3 %collective-permute-start.21 = (bf16[1024,256]{1,0:T(8,128)(2,1)S(1)}, bf16[1024,256]{1,0:T(8,128)(2,1)S(1)}, u32[]{:S(2)}, u32[]{:S(2)}) collective-permute-start(bf16[1024,256]{1,0:T(8,128)(2,1)S(1)} %get-tuple-element.92), channel_id=1, source_target_pairs={{8,16},{12,20},{16,8},{20,12},{24,32},{28,36},{32,24},{36,28},{40,... | collective-permute-start | bytes 1572872 | tf_op jit(solution)/shard_map/ppermute | solution.py:27
  69.2 14.2 %collective-permute-start.22 = (bf16[1024,256]{1,0:T(8,128)(2,1)S(1)}, bf16[1024,256]{1,0:T(8,128)(2,1)S(1)}, u32[]{:S(2)}, u32[]{:S(2)}) collective-permute-start(bf16[1024,256]{1,0:T(8,128)(2,1)S(1)} %get-tuple-element.93), channel_id=1, source_target_pairs={{0,8},{4,12},{8,0},{12,4},{16,24},{20,28},{24,16},{28,20},{32,40},... | collective-permute-start | bytes 1572872 | tf_op jit(solution)/shard_map/ppermute | solution.py:16
  69.3 25.3 %collective-permute-start.17 = (bf16[1024,256]{1,0:T(8,128)(2,1)S(1)}, bf16[1024,256]{1,0:T(8,128)(2,1)S(1)}, u32[]{:S(2)}, u32[]{:S(2)}) collective-permute-start(bf16[1024,256]{1,0:T(8,128)(2,1)S(1)} %get-tuple-element.85), channel_id=1, source_target_pairs={{8,16},{12,20},{16,8},{20,12},{24,32},{28,36},{32,24},{36,28},{40,... | collective-permute-start | bytes 1572872 | tf_op jit(solution)/shard_map/ppermute | solution.py:27
  74.0 20.7 %collective-permute-start.18 = (bf16[1024,256]{1,0:T(8,128)(2,1)S(1)}, bf16[1024,256]{1,0:T(8,128)(2,1)S(1)}, u32[]{:S(2)}, u32[]{:S(2)}) collective-permute-start(bf16[1024,256]{1,0:T(8,128)(2,1)S(1)} %get-tuple-element.86), channel_id=1, source_target_pairs={{0,8},{4,12},{8,0},{12,4},{16,24},{20,28},{24,16},{28,20},{32,40},... | collective-permute-start | bytes 1572872 | tf_op jit(solution)/shard_map/ppermute | solution.py:16
  (14 other events, 137.6 us)

commit v2 on v1

--- a/solution.py
+++ b/solution.py
@@ -124,6 +124,8 @@
 
 
 def leaf_weight_body(rm, c, out_c, out_ct):
+    rm.wait()
+    c.wait()
     select = selector_t(rm[...])
     size = 256
 
@@ -206,20 +208,28 @@
         out_load[block(((front >> 2) & 1) * 4 + place, n3), :] = piece[2 * n2 + n3 :, block(core, half)]
 
 
-def first_body(mine, other, inv, d, load2, out_rhs, out_term):
+def first_body(mine, other, inv, d, load2, out_rhs, *terms):
+    rhs = (mine[...] + other[...].astype(F32)).astype(BF16)
+    out_rhs[...] = rhs
+    y = mm(inv[...], rhs).astype(BF16)
+    term = (load2[...].astype(F32) - mm(d[...], y)).astype(BF16)
+    size = term.shape[1] // len(terms)
+    for i, out in enumerate(terms):
+        out[...] = term[:, i * size : (i + 1) * size]
+
+
+def second_body(part, mine, other, inv, e, load3, out_rhs, out_term):
+    size = mine.shape[1]
     rhs = (mine[...].astype(F32) + other[...].astype(F32)).astype(BF16)
     out_rhs[...] = rhs
     y = mm(inv[...], rhs).astype(BF16)
-    out_term[...] = (load2[...].astype(F32) - mm(d[...], y)).astype(BF16)
-
-
-def second_body(mine, other, inv, e, load3, out_rhs, out_term):
-    first_body(mine, other, inv, e, load3, out_rhs, out_term)
-
-
-def down_body(mine, other, third_near, third_far, e_t, inv2, rhs2, d_t, inv1, rhs1, out1, own2, away2, own3, away3, out3, out2):
+    out_term[...] = (load3[:, part * size : (part + 1) * size].astype(F32) - mm(e[...], y)).astype(BF16)
+
+
+def down_body(part, mine, other, third_near, third_far, e_t, inv2, rhs2, d_t, inv1, rhs1, out1, own2, away2, own3, away3, out3, out2):
     front = lax.axis_index("front")
     bit = (front >> 2) & 1
+    size = mine.shape[1]
     rhs = (mine[...].astype(F32) + other[...].astype(F32)).astype(BF16)
     rows = third_near.shape[0]
     out3[block(bit, rows), :] = mm(third_near[...], rhs).astype(BF16)
@@ -227,21 +237,22 @@
     left = (rhs2[...].astype(F32) - mm(e_t[...], out3[...])).astype(BF16)
     sol = mm(inv2[...], left).astype(BF16)
     out2[...] = sol
-    left = (rhs1[...].astype(F32) - mm(d_t[...], sol)).astype(BF16)
+    left = (rhs1[:, part * size : (part + 1) * size].astype(F32) - mm(d_t[...], sol)).astype(BF16)
     out1[...] = mm(inv1[...], left).astype(BF16)
     for own, away, whole, place in ((own2, away2, out2, front & 3), (own3, away3, out3, front & 7)):
         own[...] = whole[block(place, own.shape[0]), :]
         away[...] = whole[block(place ^ 1, own.shape[0]), :]
 
 
-def stage_body(c_t, b, surface, own, up_top, up_low, down_top, down_low, far_top, far_low, out_ct, out_b, out_surface, out_factor, sems):
-    col = lax.axis_index("col")
-    size = up_top.shape[0]
-    pairs = [(c_t, out_ct), (b, out_b)]
-    for piece, place in ((own, 0), (up_top, 6), (up_low, 7), (down_top, 2), (down_low, 3), (far_top, 4), (far_low, 5)):
-        rows = pl.ds(pl.multiple_of(((2 * col + place) & 7) * size, size), piece.shape[0])
-        pairs.append((piece, out_factor.at[rows, :]))
-    pairs.append((surface, out_surface))
+def merge_body(second_a, second_b, third_a, third_b, out):
+    rows, size = second_a.shape
+    out[:rows, :size] = second_a[...]
+    out[:rows, size:] = second_b[...]
+    out[rows:, :size] = third_a[...]
+    out[rows:, size:] = third_b[...]
+
+
+def copy_all(pairs, sems):
     copies = [pltpu.make_async_copy(x, y, sems.at[i]) for i, (x, y) in enumerate(pairs)]
     for copy in copies:
         copy.start()
@@ -249,23 +260,51 @@
         copy.wait()
 
 
+def stage_body(b, surface, out_b, out_surface, sems):
+    copy_all([(b, out_b), (surface, out_surface)], sems)
+
+
+def factor_body(own, up_top, up_low, down_top, down_low, far_top, far_low, out, sems):
+    col = lax.axis_index("col")
+    size = up_top.shape[0]
+    pairs = []
+    for piece, place in ((own, 0), (up_top, 6), (up_low, 7), (down_top, 2), (down_low, 3), (far_top, 4), (far_low, 5)):
+        rows = pl.ds(pl.multiple_of(((2 * col + place) & 7) * size, size), piece.shape[0])
+        pairs.append((piece, out.at[rows, :]))
+    copy_all(pairs, sems)
+
+
+def chunk_of(core, part, size):
+    return slice((2 * core + part) * size, (2 * core + part + 1) * size)
+
+
+def store_chunks(source, out, part, size, sems):
+    stores = []
+    for i in (0, 1):
+        stores.append(
+            pltpu.make_async_copy(source.at[:, i * size : (i + 1) * size], out.at[:, chunk_of(i, part, size)], sems.at[i])
+        )
+        stores[-1].start()
+    return stores
+
+
 def volume_body(part, c_t, b, factor, surface, s_own, s_away, aim, *rest):
-    out, out_v, out_near, out_relay, out_up, out_down, left, sem = rest[-8:]
-    front = lax.axis_index("front")
-    core = front & 1
-    half = out_v.shape[1]
-    side = jnp.where(core == part, s_own[...], s_away[...])
+    out, out_v, out_near, out_relay, out_up, out_down, left, sems = rest[-8:]
+    core = lax.axis_index("front") & 1
+    size = s_own.shape[1]
+    sides = (jnp.where(core == 0, s_own[...], s_away[...]), jnp.where(core == 0, s_away[...], s_own[...]))
+    side = jnp.concatenate(sides, axis=1)
 
     def start(rows):
-        left[rows, :] = (b[rows, part * half : (part + 1) * half].astype(F32) - mm(c_t[rows, :], side)).astype(BF16)
+        load = jnp.concatenate([b[rows, chunk_of(i, part, size)] for i in (0, 1)], axis=1)
+        left[rows, :] = (load.astype(F32) - mm(c_t[rows, :], side)).astype(BF16)
 
     def solve(rows):
         out_v[rows, :] = mm(factor[rows, :], left[...]).astype(BF16)
 
     each(b.shape[0], 256, start)
     each(b.shape[0], 256, solve)
-    store = pltpu.make_async_copy(out_v, out.at[:, part * half : (part + 1) * half], sem)
-    store.start()
+    stores = store_chunks(out_v, out, part, size, sems)
     inner = 1 - 2 * core
 
     def tiles(rows):
@@ -279,7 +318,8 @@
             out[rows, :] = jnp.where(one == offset, c_one, jnp.where(two == offset, c_two, zero))
 
     each(surface.shape[1], 256, tiles)
-    store.wait()
+    for store in stores:
+        store.wait()
 
 
 def sum_body(up, down, relay, out_inner, out_outer):
@@ -296,14 +336,20 @@
                 to_down[...] = down[...] + relay[...] if which == 1 else down[...]
 
 
-def outs_body(first, first_away, second, second_away, third, third_away, out1, out2, out3, t1, t2, t3, sems):
+def outs_body(first_a, first_b, first_away_a, first_away_b, second_a, second_b, third_a, third_b, away, out1, out2, out3, t1, t2, t3, sems):
     core = lax.axis_index("front") & 1
-    half = first.shape[1]
+    size = first_a.shape[1]
     rows = block(core, t1.shape[0])
+    n2 = t2.shape[0]
     copies = []
-    for i, (own, away, out, total) in enumerate(((first.at[rows, :], first_away.at[rows, :], out1, t1), (second, second_away, out2, t2), (third, third_away, out3, t3))):
-        total[:, block(core, half)] = own[...]
-        total[:, block(1 - core, half)] = away[...]
+    for i, (out, total, own, theirs) in enumerate((
+        (out1, t1, (first_a.at[rows, :], first_b.at[rows, :]), (first_away_a.at[rows, :], first_away_b.at[rows, :])),
+        (out2, t2, (second_a, second_b), (away.at[:n2, :size], away.at[:n2, size:])),
+        (out3, t3, (third_a, third_b), (away.at[n2:, :size], away.at[n2:, size:])),
+    )):
+        for part in (0, 1):
+            total[:, block(2 * core + part, size)] = own[part][...]
+            total[:, block(2 * (1 - core) + part, size)] = theirs[part][...]
         copies.append(pltpu.make_async_copy(total, out, sems.at[i]))
         copies[-1].start()
     for copy in copies:
@@ -318,8 +364,7 @@
 
 
 def finish_body(part, own, near, back, ahead, *rest):
-    out, total, sem = rest[-3:]
-    half = own.shape[1]
+    out, total, sems = rest[-3:]
 
     def tiles(rows):
         total[rows, :] = (
@@ -327,9 +372,8 @@
         ).astype(BF16)
 
     each(own.shape[0], 256, tiles)
-    store = pltpu.make_async_copy(total, out.at[:, part * half : (part + 1) * half], sem)
-    store.start()
-    store.wait()
+    for store in store_chunks(total, out, part, own.shape[1] // 2, sems):
+        store.wait()
 
 
 VMEM = pl.BlockSpec(memory_space=pltpu.VMEM)
@@ -345,25 +389,23 @@
         out_shape=[jax.ShapeDtypeStruct(shape.shape, BF16)] + extra_outs[1:],
         in_specs=[VMEM] * len(args) + [SMEM] * len(scalars) + [HBM] * len(more),
         out_specs=[HBM] + [VMEM] * len(extra_outs[1:]),
-        scratch_shapes=scratch + [pltpu.SemaphoreType.DMA],
+        scratch_shapes=scratch + [pltpu.SemaphoreType.DMA((2,))],
         input_output_aliases={len(args) + len(scalars): 0} if more else {},
         compiler_params=pltpu.CompilerParams(vmem_limit_bytes=12 << 20),
         cost_estimate=pl.CostEstimate(flops=int(flops), bytes_accessed=8 << 20, transcendentals=0),
     )(*args, *scalars, *more)
 
 
-def stage(args):
-    shapes = [args[0].shape, args[1].shape, args[2].shape, (args[0].shape[0],) * 2]
+def stage(body, shapes, args):
     args = [pltpu.with_memory_space_constraint(a, pltpu.HBM) for a in args]
     return pl.pallas_call(
-        stage_body,
+        body,
         out_shape=[jax.ShapeDtypeStruct(x, BF16) for x in shapes],
         in_specs=[HBM] * len(args),
-        out_specs=[VMEM] * 4,
+        out_specs=[VMEM] * len(shapes),
         scratch_shapes=[pltpu.SemaphoreType.DMA((len(args),))],
-        compiler_params=pltpu.CompilerParams(vmem_limit_bytes=12 << 20),
-        cost_estimate=pl.CostEstimate(flops=0, bytes_accessed=10 << 20, transcendentals=0),
-        name="stage",
+        compiler_params=pltpu.CompilerParams(vmem_limit_bytes=2 << 20),
+        cost_estimate=pl.CostEstimate(flops=0, bytes_accessed=8 << 20, transcendentals=0),
     )(*args)
 
 
@@ -412,7 +454,7 @@
     pack1 = flip(pack_x, 1)
     away_c = flip(pack_c, 1)
     leaf_c, leaf_ct = kernel(
-        leaf_weight_body, [((order, full), BF16), ((full, order), BF16)], (leaf_rowmap, leaf_coupling)
+        leaf_weight_body, [((order, full), BF16), ((full, order), BF16)], (leaf_rowmap, leaf_coupling), fetched=range(2)
     )
     first_d, first_dt, first_inv, load2 = kernel(
         first_weight_body, [square, square, square, column], (pack_c, away_c, load_second)
@@ -429,18 +471,34 @@
     (other,) = kernel(other_body, [column], (up_low, down_top, far_top, far_low, leaf_load, leaf_c, near_other))
     other = flip(other, 1)
     (mine,) = kernel(mine_body, [((order, half), F32)], (up_low, down_top, far_top, far_low, leaf_load, leaf_c, near_mine))
-    rhs_first, term = kernel(first_body, [column] * 2, (mine, other, first_inv, first_d, load2))
-    away = flip(term, 2)
-    rhs_second, term = kernel(second_body, [column] * 2, (term, away, second_inv, second_e, load3))
-    away = flip(term, 6)
-    staged = stage((leaf_ct, leaf_load, surface_coupling, leaf_inverse, up_top, up_low, down_top, down_low, far_top, far_low))
-    sol_first, second_own, second_away, third_own, third_away = kernel(
-        down_body,
-        [column, ((n2, half), BF16), ((n2, half), BF16), ((n3, half), BF16), ((n3, half), BF16)],
-        (term, away, third_near, third_far, second_et, second_inv, rhs_second, first_dt, first_inv, rhs_first),
-        scratch=[pltpu.VMEM(*column)] * 2,
-    )
-    sol_away = flip(sol_first, 1)
+    piece = ((order, half // 2), BF16)
+    rhs_first, *terms = kernel(first_body, [column, piece, piece], (mine, other, first_inv, first_d, load2))
+    aways = []
+    for part in range(2):
+        aways.append(flip(terms[part], 2))
+    load, surface = stage(stage_body, [leaf_load.shape, surface_coupling.shape], (leaf_load, surface_coupling))
+    (factor,) = stage(factor_body, [(full, full)], (leaf_inverse, up_top, up_low, down_top, down_low, far_top, far_low))
+    rhs_second, aways_second, terms_second = [], [], []
+    for part in range(2):
+        rhs, term = kernel(
+            functools.partial(second_body, part),
+            [piece, piece],
+            (terms[part], aways[part], second_inv, second_e, load3),
+        )
+        aways_second.append(flip(term, 6))
+        rhs_second.append(rhs)
+        terms_second.append(term)
+    firsts, firsts_away, small = [], [], []
+    for part in range(2):
+        first, *rest = kernel(
+            functools.partial(down_body, part),
+            [piece] + [((n, half // 2), BF16) for n in (n2, n2, n3, n3)],
+            (terms_second[part], aways_second[part], third_near, third_far, second_et, second_inv, rhs_second[part], first_dt, first_inv, rhs_first),
+            scratch=[pltpu.VMEM(*piece)] * 2,
+        )
+        firsts_away.append(flip(first, 1))
+        firsts.append(first)
+        small.append(rest)
 
     tail = []
     out_volume = out_tiles = None
@@ -449,7 +507,7 @@
     for part in range(2):
         out_volume, volume, near, relay, ahead_sum, back_sum = halves(
             functools.partial(volume_body, part),
-            (staged[0], staged[1], staged[3], staged[2], sol_first, sol_away, aim),
+            (leaf_ct, load, factor, surface, firsts[part], firsts_away[part], aim),
             (),
             [part_shape] * 6,
             [part_scratch],
@@ -461,26 +519,26 @@
         from_outer = swap_next(outer)
         from_inner = flip(inner, 2)
         near = flip(near, 1)
-        (c_own,) = kernel(own_body, [((full, half), BF16)], (staged[2], volume))
+        (c_own,) = kernel(own_body, [((full, half), BF16)], (surface, volume))
         tail.append((c_own, near, from_outer, from_inner))
     for part, terms in enumerate(tail):
         (out_tiles,) = halves(
             functools.partial(finish_body, part), terms, (), [part_shape], [part_scratch], out_tiles, 1e6
         )
 
-    second_away = flip(second_away, 1)
-    third_away = flip(third_away, 1)
+    (away,) = kernel(merge_body, [((n2 + n3, half), BF16)], (small[0][1], small[1][1], small[0][3], small[1][3]), 1e6)
+    away = flip(away, 1)
     shapes = [(n1, panel), (n2, panel), (n3, panel)]
     out_first, out_second, out_third = pl.pallas_call(
         outs_body,
         out_shape=[jax.ShapeDtypeStruct(x, BF16) for x in shapes],
-        in_specs=[VMEM] * 6,
+        in_specs=[VMEM] * 9,
         out_specs=[HBM] * 3,
         scratch_shapes=[pltpu.VMEM(x, BF16) for x in shapes] + [pltpu.SemaphoreType.DMA((3,))],
         compiler_params=pltpu.CompilerParams(vmem_limit_bytes=4 << 20),
         cost_estimate=pl.CostEstimate(flops=0, bytes_accessed=1 << 20, transcendentals=0),
         name="outs",
-    )(sol_first, sol_away, second_own, second_away, third_own, third_away)
+    )(*firsts, *firsts_away, small[0][0], small[1][0], small[0][2], small[1][2], away)
     return (out_volume, out_tiles, out_first, out_second, out_third)
 
 

time: 96.7 us -> 95.1 us (0.983)
  waiting for transfers between devices: 29 us -> 21.5 us
  Pallas kernels: 30.4 us -> 34.7 us
  starting transfers between devices: 31.3 us -> 34.8 us
  local copies, waits for them, and re-layouts: 3.92 us -> 2.01 us
    ppermute x17 -> x19, waiting for transfers between devices: 10.5 us -> 3.22 us  [flip(): return lax.ppermute(x, 'front', [(i, i ^ mask) for i in range(count)])]
    pallas_call x14 -> x17, Pallas kernels: 15.3 us -> 19 us  [kernel(): pl.pallas_call(run, out_shape=[jax.ShapeDtypeStruct(s, t) for s, t in out...]
    ppermute x17 -> x19, starting transfers between devices: 15.8 us -> 19.3 us  [flip(): return lax.ppermute(x, 'front', [(i, i ^ mask) for i in range(count)])]
    unnamed x27 -> x21, local copies, waits for them, and re-layouts: 2.73 us -> 0.82 us
    pallas_call x1 -> x2, Pallas kernels: 4.15 us -> 4.71 us  [stage(): pl.pallas_call(body, out_shape=[jax.ShapeDtypeStruct(x, BF16) for x in sh...]
  transfers between devices with their start and end apart: 25 -> 27, of which waited for: 6 -> 5; matrix products, arithmetic and copies ran while one was open for 1% -> 1% of each run, Pallas kernels for 25% -> 36%
where the time goes in v2:
time: 95.1 us; the launch traced here: 94.3 us
  starting transfers between devices  34.8 us (37%)
  Pallas kernels  34.7 us (36%)
  waiting for transfers between devices  21.5 us (23%)
  local copies, waits for them, and re-layouts  2.01 us (2%)
  between operations  1.23 us (1%)
    ppermute x19, starting transfers between devices, flip(): return lax.ppermute(x, 'front', [(i, i ^ mask) for i in range(count)])  19.3 us
    pallas_call x17, Pallas kernels, kernel(): pl.pallas_call(run, out_shape=[jax.ShapeDtypeStruct(s, t) for s, t in out...  19 us
    ppermute x2, waiting for transfers between devices, swap_next(): lax.ppermute(x, 'front', [(i, j) for i, j in pairs if 0 <= j < count])  16.2 us
    pallas_call x4, Pallas kernels, halves(): pl.pallas_call(body, out_shape=[jax.ShapeDtypeStruct(shape.shape, BF16)]...  10.2 us
    ppermute x2, starting transfers between devices, swap_next(): lax.ppermute(x, 'front', [(i, j) for i, j in pairs if 0 <= j < count])  8.6 us
    ppermute x6, starting transfers between devices, shift(): lax.ppermute(x, axis, [(i, (i + steps) % count) for i in range(count)])  6.9 us
    pallas_call x2, Pallas kernels, stage(): pl.pallas_call(body, out_shape=[jax.ShapeDtypeStruct(x, BF16) for x in sh...  4.71 us
    ppermute x19, waiting for transfers between devices, flip(): return lax.ppermute(x, 'front', [(i, i ^ mask) for i in range(count)])  3.22 us
  transfers between devices with their start and end apart: 27, of which 5 were waited for; matrix products, arithmetic and copies ran while one was open for 1% of the time, Pallas kernels for 36%

profile of v2, /device:TPU:129, one launch (start us, length us, event | category | flops | bytes accessed | tf_op | source)
XLA Modules:
  0.0 94.3 jit_solution(6189197783706737406)
XLA Ops:
  3.2 1.5 %collective-permute-start.3 = (bf16[128,1024]{1,0:T(8,128)(2,1)S(1)}, bf16[128,1024]{1,0:T(8,128)(2,1)S(1)}, u32[]{:S(2)}, u32[]{:S(2)}) collective-permute-start(bf16[128,1024]{1,0:T(8,128)(2,1)S(1)} %get-tuple-element.113), channel_id=1, source_target_pairs={{0,3},{1,0},{2,1},{3,2},{4,7},{5,4},{6,5},{7,6},{8,11},{9,8},{10,9... | collective-permute-start | bytes 786440 | tf_op jit(solution)/shard_map/ppermute | solution.py:21
  5.5 2.8 %shard_map.197 = (bf16[384,512]{1,0:T(8,128)(2,1)S(1)}, bf16[640,512]{1,0:T(8,128)(2,1)S(1)}, s32[8,128]{1,0:T(8,128)S(1)}) custom-call(s32[32,512]{1,0:T(8,128)} %refs_0_.5, s32[16,512]{1,0:T(8,128)} %refs_1_.3, bf16[512,256]{1,0:T(8,128)(2,1)} %refs_2_.2, bf16[512,128]{1,0:T(8,128)(2,1)} %refs_3_.3, bf16[256,512]{1,0:T(8,128)(2,1)} %refs_4_.5, ...), custom_call_target="tpu_custom_call" | custom-call | flops 1000000000 | bytes 1146880 | tf_op jit(solution)/shard_map/pallas_call | solution.py:75
  9.7 1.7 %collective-permute-start.7 = (bf16[640,512]{1,0:T(8,128)(2,1)S(1)}, bf16[640,512]{1,0:T(8,128)(2,1)S(1)}, u32[]{:S(2)}, u32[]{:S(2)}) collective-permute-start(bf16[640,512]{1,0:T(8,128)(2,1)S(1)} %get-tuple-element.65.refs_0_), channel_id=1, source_target_pairs={{0,4},{4,0},{8,12},{12,8},{16,20},{20,16},{24,28},{28,24},{32,36},... | collective-permute-start | bytes 1966088 | tf_op jit(solution)/shard_map/ppermute | solution.py:16
  11.4 2.6 %collective-permute-start.2 = (bf16[128,1024]{1,0:T(8,128)(2,1)S(1)}, bf16[128,1024]{1,0:T(8,128)(2,1)S(1)}, u32[]{:S(2)}, u32[]{:S(2)}) collective-permute-start(bf16[128,1024]{1,0:T(8,128)(2,1)S(1)} %get-tuple-element.114), channel_id=1, source_target_pairs={{0,3},{1,0},{2,1},{3,2},{4,7},{5,4},{6,5},{7,6},{8,11},{9,8},{10,9... | collective-permute-start | bytes 786440 | tf_op jit(solution)/shard_map/ppermute | solution.py:21
  14.0 2.1 %collective-permute-done.1.up_low.refs_0_ = bf16[128,1024]{1,0:T(8,128)(2,1)S(1)} collective-permute-done((bf16[128,1024]{1,0:T(8,128)(2,1)S(1)}, bf16[128,1024]{1,0:T(8,128)(2,1)S(1)}, u32[]{:S(2)}, u32[]{:S(2)}) %collective-permute-start.1) | collective-permute-done | bytes 262176 | tf_op jit(solution)/shard_map/ppermute | solution.py:21
  16.1 1.4 %collective-permute-start.5 = (bf16[128,1024]{1,0:T(8,128)(2,1)S(1)}, bf16[128,1024]{1,0:T(8,128)(2,1)S(1)}, u32[]{:S(2)}, u32[]{:S(2)}) collective-permute-start(bf16[128,1024]{1,0:T(8,128)(2,1)S(1)} %collective-permute-done.3.down_low.refs_2_), channel_id=1, source_target_pairs={{0,3},{1,0},{2,1},{3,2},{4,7},{5,4},{6,5},{7,6},{8,11},{9,8},{10,9... | collective-permute-start | bytes 786440 | tf_op jit(solution)/shard_map/ppermute | solution.py:21
  17.5 3.5 %shard_map.191 = (bf16[512,1024]{1,0:T(8,128)(2,1)S(1)}, bf16[1024,512]{1,0:T(8,128)(2,1)S(1)}) custom-call(s32[1,512]{1,0:T(1,128)} %refs_0_.3, bf16[512,1024]{1,0:T(8,128)(2,1)} %refs_1_.2), custom_call_target="tpu_custom_call" | custom-call | flops 1000000000 | bytes 1050624 | tf_op jit(solution)/shard_map/pallas_call | solution.py:75
  21.0 1.8 %shard_map.194 = (f32[512,256]{1,0:T(8,128)S(1)}, f32[512,256]{1,0:T(8,128)S(1)}) custom-call(bf16[256,1024]{1,0:T(8,128)(2,1)S(1)} %copy-done.5, bf16[128,1024]{1,0:T(8,128)(2,1)S(1)} %collective-permute-done.up_top.refs_1_, bf16[128,1024]{1,0:T(8,128)(2,1)S(1)} %collective-permute-done.3.down_low.refs_2_, bf16[1024,512]{1,0:T(8,128)(2,1)S(1)} %copy-done, ...), custom_call_target="tpu_custom_call" | custom-call | flops 2000000000 | bytes 3407872 | tf_op jit(solution)/shard_map/pallas_call | solution.py:75
  22.8 3.0 %collective-permute-start.9 = (bf16[384,512]{1,0:T(8,128)(2,1)S(1)}, bf16[384,512]{1,0:T(8,128)(2,1)S(1)}, u32[]{:S(2)}, u32[]{:S(2)}) collective-permute-start(bf16[384,512]{1,0:T(8,128)(2,1)S(1)} %get-tuple-element.70.refs_0_), channel_id=1, source_target_pairs={{0,4},{4,0},{8,12},{12,8},{16,20},{20,16},{24,28},{28,24},{32,36},... | collective-permute-start | bytes 1179656 | tf_op jit(solution)/shard_map/ppermute | solution.py:16
  31.5 1.9 %collective-permute-start.13 = (bf16[256,512]{1,0:T(8,128)(2,1)S(1)}, bf16[256,512]{1,0:T(8,128)(2,1)S(1)}, u32[]{:S(2)}, u32[]{:S(2)}) collective-permute-start(bf16[256,512]{1,0:T(8,128)(2,1)S(1)} %get-tuple-element.75.refs_2_), channel_id=1, source_target_pairs={{0,24},{4,28},{8,16},{12,20},{16,8},{20,12},{24,0},{28,4},{32,56},... | collective-permute-start | bytes 786440 | tf_op jit(solution)/shard_map/ppermute | solution.py:16
  35.6 2.6 %collective-permute-start.16 = (bf16[512,128]{1,0:T(8,128)(2,1)S(1)}, bf16[512,128]{1,0:T(8,128)(2,1)S(1)}, u32[]{:S(2)}, u32[]{:S(2)}) collective-permute-start(bf16[512,128]{1,0:T(8,128)(2,1)S(1)} %get-tuple-element.83.refs_0_), channel_id=1, source_target_pairs={{0,24},{4,28},{8,16},{12,20},{16,8},{20,12},{24,0},{28,4},{32,56},... | collective-permute-start | bytes 393224 | tf_op jit(solution)/shard_map/ppermute | solution.py:16
  39.0 2.1 %collective-permute-start.12 = (bf16[512,128]{1,0:T(8,128)(2,1)S(1)}, bf16[512,128]{1,0:T(8,128)(2,1)S(1)}, u32[]{:S(2)}, u32[]{:S(2)}) collective-permute-start(bf16[512,128]{1,0:T(8,128)(2,1)S(1)} %get-tuple-element.74.refs_0_), channel_id=1, source_target_pairs={{0,24},{4,28},{8,16},{12,20},{16,8},{20,12},{24,0},{28,4},{32,56},... | collective-permute-start | bytes 393224 | tf_op jit(solution)/shard_map/ppermute | solution.py:16
  41.0 2.0 %collective-permute-done.16.refs_1_ = bf16[512,128]{1,0:T(8,128)(2,1)S(1)} collective-permute-done((bf16[512,128]{1,0:T(8,128)(2,1)S(1)}, bf16[512,128]{1,0:T(8,128)(2,1)S(1)}, u32[]{:S(2)}, u32[]{:S(2)}) %collective-permute-start.16) | collective-permute-done | bytes 131104 | tf_op jit(solution)/shard_map/ppermute | solution.py:16
  43.0 1.6 %shard_map.204 = (bf16[512,128]{1,0:T(8,128)(2,1)S(1)}, bf16[128,128]{1,0:T(8,128)(2,1)S(1)}, bf16[128,128]{1,0:T(8,128)(2,1)S(1)}, bf16[64,128]{1,0:T(8,128)(2,1)S(1)}, bf16[64,128]{1,0:T(8,128)(2,1)S(1)}) custom-call(bf16[512,128]{1,0:T(8,128)(2,1)S(1)} %get-tuple-element.83.refs_0_, bf16[512,128]{1,0:T(8,128)(2,1)S(1)} %collective-permute-done.16.refs_1_, ...), custom_call_target="tpu_custom_call" | custom-call | flops 1000000000 | bytes 3276800 | tf_op jit(solution)/shard_map/pallas_call | solution.py:75
  44.7 2.3 %collective-permute-start.17 = (bf16[512,128]{1,0:T(8,128)(2,1)S(1)}, bf16[512,128]{1,0:T(8,128)(2,1)S(1)}, u32[]{:S(2)}, u32[]{:S(2)}) collective-permute-start(bf16[512,128]{1,0:T(8,128)(2,1)S(1)} %get-tuple-element.85.s_own.first_a), channel_id=1, source_target_pairs={{0,4},{4,0},{8,12},{12,8},{16,20},{20,16},{24,28},{28,24},{32,36},... | collective-permute-start | bytes 393224 | tf_op jit(solution)/shard_map/ppermute | solution.py:16
  46.9 3.1 %shard_map.192 = (bf16[1024,512]{1,0:T(8,128)(2,1)S(1)}, bf16[3,1024,1024]{2,1,0:T(8,128)(2,1)S(1)}) custom-call(bf16[1024,512]{1,0:T(8,128)(2,1)} %refs_4_.4, bf16[3,1024,1024]{2,1,0:T(8,128)(2,1)} %surface.1), custom_call_target="tpu_custom_call" | custom-call | bytes 8388608 | tf_op jit(solution)/shard_map/pallas_call | solution.py:401
  50.1 1.6 %shard_map.193.factor = bf16[1024,1024]{1,0:T(8,128)(2,1)S(1)} custom-call(bf16[256,1024]{1,0:T(8,128)(2,1)} %refs_0_.4, bf16[128,1024]{1,0:T(8,128)(2,1)} %copy-done.6, bf16[128,1024]{1,0:T(8,128)(2,1)} %copy-done.1, bf16[128,1024]{1,0:T(8,128)(2,1)} %copy-done.2, bf16[128,1024]{1,0:T(8,128)(2,1)} %copy-done.7, bf16[128,1024]{1,0:T(8,128)(2,1)} %copy-done.3, ...), custom_call_target="tpu_custom_call" | custom-call | bytes 8388608 | tf_op jit(solution)/shard_map/pallas_call | solution.py:401
  51.7 1.7 %shard_map.202 = (bf16[512,128]{1,0:T(8,128)(2,1)S(1)}, bf16[128,128]{1,0:T(8,128)(2,1)S(1)}, bf16[128,128]{1,0:T(8,128)(2,1)S(1)}, bf16[64,128]{1,0:T(8,128)(2,1)S(1)}, bf16[64,128]{1,0:T(8,128)(2,1)S(1)}) custom-call(bf16[512,128]{1,0:T(8,128)(2,1)S(1)} %get-tuple-element.74.refs_0_, bf16[512,128]{1,0:T(8,128)(2,1)S(1)} %collective-permute-done.12.refs_1_, ...), custom_call_target="tpu_custom_call" | custom-call | flops 1000000000 | bytes 3276800 | tf_op jit(solution)/shard_map/pallas_call | solution.py:75
  53.4 4.0 %shard_map.205 = (bf16[1024,512]{1,0:T(8,128)(2,1)}, bf16[1024,256]{1,0:T(8,128)(2,1)S(1)}, bf16[1024,256]{1,0:T(8,128)(2,1)S(1)}, bf16[1024,256]{1,0:T(8,128)(2...) custom-call(bf16[1024,512]{1,0:T(8,128)(2,1)S(1)} %get-tuple-element.59.c_t, ...), custom_call_target="tpu_custom_call" | custom-call | flops 3000000000 | bytes 8388608 | tf_op jit(solution)/shard_map/pallas_call | solution.py:387
  58.1 4.0 %shard_map.206 = (bf16[1024,512]{1,0:T(8,128)(2,1)}, bf16[1024,256]{1,0:T(8,128)(2,1)S(1)}, bf16[1024,256]{1,0:T(8,128)(2,1)S(1)}, bf16[1024,256]{1,0:T(8,128)(2...) custom-call(bf16[1024,512]{1,0:T(8,128)(2,1)S(1)} %get-tuple-element.59.c_t, ...), custom_call_target="tpu_custom_call", output_to_operand_aliasing={{0}: (7, {})} | custom-call | flops 3000000000 | bytes 8388608 | tf_op jit(solution)/shard_map/pallas_call | solution.py:387
  63.4 3.3 %collective-permute-start.24 = (bf16[1024,256]{1,0:T(8,128)(2,1)S(1)}, bf16[1024,256]{1,0:T(8,128)(2,1)S(1)}, u32[]{:S(2)}, u32[]{:S(2)}) collective-permute-start(bf16[1024,256]{1,0:T(8,128)(2,1)S(1)} %get-tuple-element.100), channel_id=1, source_target_pairs={{8,16},{12,20},{16,8},{20,12},{24,32},{28,36},{32,24},{36,28},{40,... | collective-permute-start | bytes 1572872 | tf_op jit(solution)/shard_map/ppermute | solution.py:27
  66.9 5.4 %collective-permute-start.20 = (bf16[1024,256]{1,0:T(8,128)(2,1)S(1)}, bf16[1024,256]{1,0:T(8,128)(2,1)S(1)}, u32[]{:S(2)}, u32[]{:S(2)}) collective-permute-start(bf16[1024,256]{1,0:T(8,128)(2,1)S(1)} %get-tuple-element.93), channel_id=1, source_target_pairs={{8,16},{12,20},{16,8},{20,12},{24,32},{28,36},{32,24},{36,28},{40,... | collective-permute-start | bytes 1572872 | tf_op jit(solution)/shard_map/ppermute | solution.py:27
  75.7 6.1 %collective-permute-done.24.back = bf16[1024,256]{1,0:T(8,128)(2,1)S(1)} collective-permute-done((bf16[1024,256]{1,0:T(8,128)(2,1)S(1)}, bf16[1024,256]{1,0:T(8,128)(2,1)S(1)}, u32[]{:S(2)}, u32[]{:S(2)}) %collective-permute-start.24) | collective-permute-done | bytes 524320 | tf_op jit(solution)/shard_map/ppermute | solution.py:27
  82.9 10.1 %collective-permute-done.20.back = bf16[1024,256]{1,0:T(8,128)(2,1)S(1)} collective-permute-done((bf16[1024,256]{1,0:T(8,128)(2,1)S(1)}, bf16[1024,256]{1,0:T(8,128)(2,1)S(1)}, u32[]{:S(2)}, u32[]{:S(2)}) %collective-permute-start.20) | collective-permute-done | bytes 524320 | tf_op jit(solution)/shard_map/ppermute | solution.py:27
  (76 shorter events, 21.0 us)
Async XLA Ops:
  1.9 9.6 %collective-permute-start = (bf16[128,1024]{1,0:T(8,128)(2,1)S(1)}, bf16[128,1024]{1,0:T(8,128)(2,1)S(1)}, u32[]{:S(2)}, u32[]{:S(2)}) collective-permute-start(bf16[128,1024]{1,0:T(8,128)(2,1)S(1)} %get-tuple-element.114), channel_id=1, source_target_pairs={{0,1},{1,2},{2,3},{3,0},{4,5},{5,6},{6,7},{7,4},{8,9},{9,10},{10,1... | collective-permute-start | bytes 786440 | tf_op jit(solution)/shard_map/ppermute | solution.py:21
  3.2 10.8 %collective-permute-start.3 = (bf16[128,1024]{1,0:T(8,128)(2,1)S(1)}, bf16[128,1024]{1,0:T(8,128)(2,1)S(1)}, u32[]{:S(2)}, u32[]{:S(2)}) collective-permute-start(bf16[128,1024]{1,0:T(8,128)(2,1)S(1)} %get-tuple-element.113), channel_id=1, source_target_pairs={{0,3},{1,0},{2,1},{3,2},{4,7},{5,4},{6,5},{7,6},{8,11},{9,8},{10,9... | collective-permute-start | bytes 786440 | tf_op jit(solution)/shard_map/ppermute | solution.py:21
  4.8 11.3 %collective-permute-start.1 = (bf16[128,1024]{1,0:T(8,128)(2,1)S(1)}, bf16[128,1024]{1,0:T(8,128)(2,1)S(1)}, u32[]{:S(2)}, u32[]{:S(2)}) collective-permute-start(bf16[128,1024]{1,0:T(8,128)(2,1)S(1)} %get-tuple-element.113), channel_id=1, source_target_pairs={{0,1},{1,2},{2,3},{3,0},{4,5},{5,6},{6,7},{7,4},{8,9},{9,10},{10,1... | collective-permute-start | bytes 786440 | tf_op jit(solution)/shard_map/ppermute | solution.py:21
  8.4 17.4 %collective-permute-start.10 = (bf16[384,512]{1,0:T(8,128)(2,1)S(1)}, bf16[384,512]{1,0:T(8,128)(2,1)S(1)}, u32[]{:S(2)}, u32[]{:S(2)}) collective-permute-start(bf16[384,512]{1,0:T(8,128)(2,1)S(1)} %get-tuple-element.70.refs_0_), channel_id=1, source_target_pairs={{0,8},{4,12},{8,0},{12,4},{16,24},{20,28},{24,16},{28,20},{32,40},... | collective-permute-start | bytes 1179656 | tf_op jit(solution)/shard_map/ppermute | solution.py:16
  9.7 19.2 %collective-permute-start.7 = (bf16[640,512]{1,0:T(8,128)(2,1)S(1)}, bf16[640,512]{1,0:T(8,128)(2,1)S(1)}, u32[]{:S(2)}, u32[]{:S(2)}) collective-permute-start(bf16[640,512]{1,0:T(8,128)(2,1)S(1)} %get-tuple-element.65.refs_0_), channel_id=1, source_target_pairs={{0,4},{4,0},{8,12},{12,8},{16,20},{20,16},{24,28},{28,24},{32,36},... | collective-permute-start | bytes 1966088 | tf_op jit(solution)/shard_map/ppermute | solution.py:16
  11.4 11.4 %collective-permute-start.2 = (bf16[128,1024]{1,0:T(8,128)(2,1)S(1)}, bf16[128,1024]{1,0:T(8,128)(2,1)S(1)}, u32[]{:S(2)}, u32[]{:S(2)}) collective-permute-start(bf16[128,1024]{1,0:T(8,128)(2,1)S(1)} %get-tuple-element.114), channel_id=1, source_target_pairs={{0,3},{1,0},{2,1},{3,2},{4,7},{5,4},{6,5},{7,6},{8,11},{9,8},{10,9... | collective-permute-start | bytes 786440 | tf_op jit(solution)/shard_map/ppermute | solution.py:21
  14.0 11.9 %collective-permute-start.4 = (bf16[128,1024]{1,0:T(8,128)(2,1)S(1)}, bf16[128,1024]{1,0:T(8,128)(2,1)S(1)}, u32[]{:S(2)}, u32[]{:S(2)}) collective-permute-start(bf16[128,1024]{1,0:T(8,128)(2,1)S(1)} %collective-permute-done.up_top.refs_1_), channel_id=1, source_target_pairs={{0,1},{1,2},{2,3},{3,0},{4,5},{5,6},{6,7},{7,4},{8,9},{9,10},{10,1... | collective-permute-start | bytes 786440 | tf_op jit(solution)/shard_map/ppermute | solution.py:21
  16.1 9.9 %collective-permute-start.5 = (bf16[128,1024]{1,0:T(8,128)(2,1)S(1)}, bf16[128,1024]{1,0:T(8,128)(2,1)S(1)}, u32[]{:S(2)}, u32[]{:S(2)}) collective-permute-start(bf16[128,1024]{1,0:T(8,128)(2,1)S(1)} %collective-permute-done.3.down_low.refs_2_), channel_id=1, source_target_pairs={{0,3},{1,0},{2,1},{3,2},{4,7},{5,4},{6,5},{7,6},{8,11},{9,8},{10,9... | collective-permute-start | bytes 786440 | tf_op jit(solution)/shard_map/ppermute | solution.py:21
  22.8 8.4 %collective-permute-start.9 = (bf16[384,512]{1,0:T(8,128)(2,1)S(1)}, bf16[384,512]{1,0:T(8,128)(2,1)S(1)}, u32[]{:S(2)}, u32[]{:S(2)}) collective-permute-start(bf16[384,512]{1,0:T(8,128)(2,1)S(1)} %get-tuple-element.70.refs_0_), channel_id=1, source_target_pairs={{0,4},{4,0},{8,12},{12,8},{16,20},{20,16},{24,28},{28,24},{32,36},... | collective-permute-start | bytes 1179656 | tf_op jit(solution)/shard_map/ppermute | solution.py:16
  25.8 5.4 %collective-permute-start.11 = (bf16[384,512]{1,0:T(8,128)(2,1)S(1)}, bf16[384,512]{1,0:T(8,128)(2,1)S(1)}, u32[]{:S(2)}, u32[]{:S(2)}) collective-permute-start(bf16[384,512]{1,0:T(8,128)(2,1)S(1)} %collective-permute-done.10.refs_2_), channel_id=1, source_target_pairs={{0,4},{4,0},{8,12},{12,8},{16,20},{20,16},{24,28},{28,24},{32,36},... | collective-permute-start | bytes 1179656 | tf_op jit(solution)/shard_map/ppermute | solution.py:16
  29.9 5.0 %collective-permute-start.15 = (bf16[512,128]{1,0:T(8,128)(2,1)S(1)}, bf16[512,128]{1,0:T(8,128)(2,1)S(1)}, u32[]{:S(2)}, u32[]{:S(2)}) collective-permute-start(bf16[512,128]{1,0:T(8,128)(2,1)S(1)} %get-tuple-element.82.refs_0_), channel_id=1, source_target_pairs={{0,8},{4,12},{8,0},{12,4},{16,24},{20,28},{24,16},{28,20},{32,40},... | collective-permute-start | bytes 393224 | tf_op jit(solution)/shard_map/ppermute | solution.py:16
  31.5 11.5 %collective-permute-start.13 = (bf16[256,512]{1,0:T(8,128)(2,1)S(1)}, bf16[256,512]{1,0:T(8,128)(2,1)S(1)}, u32[]{:S(2)}, u32[]{:S(2)}) collective-permute-start(bf16[256,512]{1,0:T(8,128)(2,1)S(1)} %get-tuple-element.75.refs_2_), channel_id=1, source_target_pairs={{0,24},{4,28},{8,16},{12,20},{16,8},{20,12},{24,0},{28,4},{32,56},... | collective-permute-start | bytes 786440 | tf_op jit(solution)/shard_map/ppermute | solution.py:16
  33.4 4.8 %collective-permute-start.8 = (bf16[512,128]{1,0:T(8,128)(2,1)S(1)}, bf16[512,128]{1,0:T(8,128)(2,1)S(1)}, u32[]{:S(2)}, u32[]{:S(2)}) collective-permute-start(bf16[512,128]{1,0:T(8,128)(2,1)S(1)} %get-tuple-element.69.refs_0_), channel_id=1, source_target_pairs={{0,8},{4,12},{8,0},{12,4},{16,24},{20,28},{24,16},{28,20},{32,40},... | collective-permute-start | bytes 393224 | tf_op jit(solution)/shard_map/ppermute | solution.py:16
  35.6 7.4 %collective-permute-start.16 = (bf16[512,128]{1,0:T(8,128)(2,1)S(1)}, bf16[512,128]{1,0:T(8,128)(2,1)S(1)}, u32[]{:S(2)}, u32[]{:S(2)}) collective-permute-start(bf16[512,128]{1,0:T(8,128)(2,1)S(1)} %get-tuple-element.83.refs_0_), channel_id=1, source_target_pairs={{0,24},{4,28},{8,16},{12,20},{16,8},{20,12},{24,0},{28,4},{32,56},... | collective-permute-start | bytes 393224 | tf_op jit(solution)/shard_map/ppermute | solution.py:16
  39.0 12.7 %collective-permute-start.12 = (bf16[512,128]{1,0:T(8,128)(2,1)S(1)}, bf16[512,128]{1,0:T(8,128)(2,1)S(1)}, u32[]{:S(2)}, u32[]{:S(2)}) collective-permute-start(bf16[512,128]{1,0:T(8,128)(2,1)S(1)} %get-tuple-element.74.refs_0_), channel_id=1, source_target_pairs={{0,24},{4,28},{8,16},{12,20},{16,8},{20,12},{24,0},{28,4},{32,56},... | collective-permute-start | bytes 393224 | tf_op jit(solution)/shard_map/ppermute | solution.py:16
  44.7 8.8 %collective-permute-start.17 = (bf16[512,128]{1,0:T(8,128)(2,1)S(1)}, bf16[512,128]{1,0:T(8,128)(2,1)S(1)}, u32[]{:S(2)}, u32[]{:S(2)}) collective-permute-start(bf16[512,128]{1,0:T(8,128)(2,1)S(1)} %get-tuple-element.85.s_own.first_a), channel_id=1, source_target_pairs={{0,4},{4,0},{8,12},{12,8},{16,20},{20,16},{24,28},{28,24},{32,36},... | collective-permute-start | bytes 393224 | tf_op jit(solution)/shard_map/ppermute | solution.py:16
  53.3 4.7 %collective-permute-start.14 = (bf16[512,128]{1,0:T(8,128)(2,1)S(1)}, bf16[512,128]{1,0:T(8,128)(2,1)S(1)}, u32[]{:S(2)}, u32[]{:S(2)}) collective-permute-start(bf16[512,128]{1,0:T(8,128)(2,1)S(1)} %get-tuple-element.80.s_own.first_b), channel_id=1, source_target_pairs={{0,4},{4,0},{8,12},{12,8},{16,20},{20,16},{24,28},{28,24},{32,36},... | collective-permute-start | bytes 393224 | tf_op jit(solution)/shard_map/ppermute | solution.py:16
  57.5 5.8 %collective-permute-start.23 = (bf16[1024,256]{1,0:T(8,128)(2,1)S(1)}, bf16[1024,256]{1,0:T(8,128)(2,1)S(1)}, u32[]{:S(2)}, u32[]{:S(2)}) collective-permute-start(bf16[1024,256]{1,0:T(8,128)(2,1)S(1)} %get-tuple-element.99), channel_id=1, source_target_pairs={{0,4},{4,0},{8,12},{12,8},{16,20},{20,16},{24,28},{28,24},{32,36},... | collective-permute-start | bytes 1572872 | tf_op jit(solution)/shard_map/ppermute | solution.py:16
  62.2 10.0 %collective-permute-start.22 = (bf16[1024,256]{1,0:T(8,128)(2,1)S(1)}, bf16[1024,256]{1,0:T(8,128)(2,1)S(1)}, u32[]{:S(2)}, u32[]{:S(2)}) collective-permute-start(bf16[1024,256]{1,0:T(8,128)(2,1)S(1)} %get-tuple-element.96), channel_id=1, source_target_pairs={{0,4},{4,0},{8,12},{12,8},{16,20},{20,16},{24,28},{28,24},{32,36},... | collective-permute-start | bytes 1572872 | tf_op jit(solution)/shard_map/ppermute | solution.py:16
  62.9 20.0 %collective-permute-start.18 = (bf16[1024,256]{1,0:T(8,128)(2,1)S(1)}, bf16[1024,256]{1,0:T(8,128)(2,1)S(1)}, u32[]{:S(2)}, u32[]{:S(2)}) collective-permute-start(bf16[1024,256]{1,0:T(8,128)(2,1)S(1)} %get-tuple-element.89), channel_id=1, source_target_pairs={{0,4},{4,0},{8,12},{12,8},{16,20},{20,16},{24,28},{28,24},{32,36},... | collective-permute-start | bytes 1572872 | tf_op jit(solution)/shard_map/ppermute | solution.py:16
  63.4 18.4 %collective-permute-start.24 = (bf16[1024,256]{1,0:T(8,128)(2,1)S(1)}, bf16[1024,256]{1,0:T(8,128)(2,1)S(1)}, u32[]{:S(2)}, u32[]{:S(2)}) collective-permute-start(bf16[1024,256]{1,0:T(8,128)(2,1)S(1)} %get-tuple-element.100), channel_id=1, source_target_pairs={{8,16},{12,20},{16,8},{20,12},{24,32},{28,36},{32,24},{36,28},{40,... | collective-permute-start | bytes 1572872 | tf_op jit(solution)/shard_map/ppermute | solution.py:27
  66.7 15.1 %collective-permute-start.25 = (bf16[1024,256]{1,0:T(8,128)(2,1)S(1)}, bf16[1024,256]{1,0:T(8,128)(2,1)S(1)}, u32[]{:S(2)}, u32[]{:S(2)}) collective-permute-start(bf16[1024,256]{1,0:T(8,128)(2,1)S(1)} %get-tuple-element.101), channel_id=1, source_target_pairs={{0,8},{4,12},{8,0},{12,4},{16,24},{20,28},{24,16},{28,20},{32,40},... | collective-permute-start | bytes 1572872 | tf_op jit(solution)/shard_map/ppermute | solution.py:16
  66.9 26.1 %collective-permute-start.20 = (bf16[1024,256]{1,0:T(8,128)(2,1)S(1)}, bf16[1024,256]{1,0:T(8,128)(2,1)S(1)}, u32[]{:S(2)}, u32[]{:S(2)}) collective-permute-start(bf16[1024,256]{1,0:T(8,128)(2,1)S(1)} %get-tuple-element.93), channel_id=1, source_target_pairs={{8,16},{12,20},{16,8},{20,12},{24,32},{28,36},{32,24},{36,28},{40,... | collective-permute-start | bytes 1572872 | tf_op jit(solution)/shard_map/ppermute | solution.py:27
  72.3 20.7 %collective-permute-start.21 = (bf16[1024,256]{1,0:T(8,128)(2,1)S(1)}, bf16[1024,256]{1,0:T(8,128)(2,1)S(1)}, u32[]{:S(2)}, u32[]{:S(2)}) collective-permute-start(bf16[1024,256]{1,0:T(8,128)(2,1)S(1)} %get-tuple-element.94), channel_id=1, source_target_pairs={{0,8},{4,12},{8,0},{12,4},{16,24},{20,28},{24,16},{28,20},{32,40},... | collective-permute-start | bytes 1572872 | tf_op jit(solution)/shard_map/ppermute | solution.py:16
  (13 other events, 135.0 us)

commit v3 on v2

--- a/solution.py
+++ b/solution.py
@@ -365,14 +365,15 @@
 
 def finish_body(part, own, near, back, ahead, *rest):
     out, total, sems = rest[-3:]
-
-    def tiles(rows):
+    size, tile = own.shape[1] // 2, own.shape[0] // 4
+    stores = []
+    for k in range(4):
+        rows = slice(k * tile, (k + 1) * tile)
         total[rows, :] = (
             own[rows, :].astype(F32) + near[rows, :].astype(F32) + back[rows, :].astype(F32) + ahead[rows, :].astype(F32)
         ).astype(BF16)
-
-    each(own.shape[0], 256, tiles)
-    for store in store_chunks(total, out, part, own.shape[1] // 2, sems):
+        stores += store_chunks(total.at[rows, :], out.at[rows, :], part, size, sems.at[2 * k : 2 * k + 2])
+    for store in stores:
         store.wait()
 
 
@@ -389,7 +390,7 @@
         out_shape=[jax.ShapeDtypeStruct(shape.shape, BF16)] + extra_outs[1:],
         in_specs=[VMEM] * len(args) + [SMEM] * len(scalars) + [HBM] * len(more),
         out_specs=[HBM] + [VMEM] * len(extra_outs[1:]),
-        scratch_shapes=scratch + [pltpu.SemaphoreType.DMA((2,))],
+        scratch_shapes=scratch + [pltpu.SemaphoreType.DMA((8,))],
         input_output_aliases={len(args) + len(scalars): 0} if more else {},
         compiler_params=pltpu.CompilerParams(vmem_limit_bytes=12 << 20),
         cost_estimate=pl.CostEstimate(flops=int(flops), bytes_accessed=8 << 20, transcendentals=0),

time: 95.1 us -> 95.1 us (level)
  no operation moved by 1% of the time
where the time goes in v3:
time: 95.1 us; the launch traced here: 94.3 us
  starting transfers between devices  34.8 us (37%)
  Pallas kernels  34.7 us (36%)
  waiting for transfers between devices  21.6 us (23%)
  local copies, waits for them, and re-layouts  2.01 us (2%)
  between operations  1.23 us (1%)
    ppermute x19, starting transfers between devices, flip(): return lax.ppermute(x, 'front', [(i, i ^ mask) for i in range(count)])  19.3 us
    pallas_call x17, Pallas kernels, kernel(): pl.pallas_call(run, out_shape=[jax.ShapeDtypeStruct(s, t) for s, t in out...  19 us
    ppermute x2, waiting for transfers between devices, swap_next(): lax.ppermute(x, 'front', [(i, j) for i, j in pairs if 0 <= j < count])  16.3 us
    pallas_call x4, Pallas kernels, halves(): pl.pallas_call(body, out_shape=[jax.ShapeDtypeStruct(shape.shape, BF16)]...  10.1 us
    ppermute x2, starting transfers between devices, swap_next(): lax.ppermute(x, 'front', [(i, j) for i, j in pairs if 0 <= j < count])  8.6 us
    ppermute x6, starting transfers between devices, shift(): lax.ppermute(x, axis, [(i, (i + steps) % count) for i in range(count)])  6.9 us
    pallas_call x2, Pallas kernels, stage(): pl.pallas_call(body, out_shape=[jax.ShapeDtypeStruct(x, BF16) for x in sh...  4.71 us
    ppermute x19, waiting for transfers between devices, flip(): return lax.ppermute(x, 'front', [(i, i ^ mask) for i in range(count)])  3.22 us
  transfers between devices with their start and end apart: 27, of which 5 were waited for; matrix products, arithmetic and copies ran while one was open for 1% of the time, Pallas kernels for 36%

profile of v3, /device:TPU:129, one launch (start us, length us, event | category | flops | bytes accessed | tf_op | source)
XLA Modules:
  0.0 94.3 jit_solution(14513428414290741793)
XLA Ops:
  3.2 1.5 %collective-permute-start.3 = (bf16[128,1024]{1,0:T(8,128)(2,1)S(1)}, bf16[128,1024]{1,0:T(8,128)(2,1)S(1)}, u32[]{:S(2)}, u32[]{:S(2)}) collective-permute-start(bf16[128,1024]{1,0:T(8,128)(2,1)S(1)} %get-tuple-element.113), channel_id=1, source_target_pairs={{0,3},{1,0},{2,1},{3,2},{4,7},{5,4},{6,5},{7,6},{8,11},{9,8},{10,9... | collective-permute-start | bytes 786440 | tf_op jit(solution)/shard_map/ppermute | solution.py:21
  5.5 2.8 %shard_map.197 = (bf16[384,512]{1,0:T(8,128)(2,1)S(1)}, bf16[640,512]{1,0:T(8,128)(2,1)S(1)}, s32[8,128]{1,0:T(8,128)S(1)}) custom-call(s32[32,512]{1,0:T(8,128)} %refs_0_.5, s32[16,512]{1,0:T(8,128)} %refs_1_.3, bf16[512,256]{1,0:T(8,128)(2,1)} %refs_2_.2, bf16[512,128]{1,0:T(8,128)(2,1)} %refs_3_.3, bf16[256,512]{1,0:T(8,128)(2,1)} %refs_4_.5, ...), custom_call_target="tpu_custom_call" | custom-call | flops 1000000000 | bytes 1146880 | tf_op jit(solution)/shard_map/pallas_call | solution.py:75
  9.7 1.7 %collective-permute-start.7 = (bf16[640,512]{1,0:T(8,128)(2,1)S(1)}, bf16[640,512]{1,0:T(8,128)(2,1)S(1)}, u32[]{:S(2)}, u32[]{:S(2)}) collective-permute-start(bf16[640,512]{1,0:T(8,128)(2,1)S(1)} %get-tuple-element.65.refs_0_), channel_id=1, source_target_pairs={{0,4},{4,0},{8,12},{12,8},{16,20},{20,16},{24,28},{28,24},{32,36},... | collective-permute-start | bytes 1966088 | tf_op jit(solution)/shard_map/ppermute | solution.py:16
  11.4 2.6 %collective-permute-start.2 = (bf16[128,1024]{1,0:T(8,128)(2,1)S(1)}, bf16[128,1024]{1,0:T(8,128)(2,1)S(1)}, u32[]{:S(2)}, u32[]{:S(2)}) collective-permute-start(bf16[128,1024]{1,0:T(8,128)(2,1)S(1)} %get-tuple-element.114), channel_id=1, source_target_pairs={{0,3},{1,0},{2,1},{3,2},{4,7},{5,4},{6,5},{7,6},{8,11},{9,8},{10,9... | collective-permute-start | bytes 786440 | tf_op jit(solution)/shard_map/ppermute | solution.py:21
  14.0 2.1 %collective-permute-done.1.up_low.refs_0_ = bf16[128,1024]{1,0:T(8,128)(2,1)S(1)} collective-permute-done((bf16[128,1024]{1,0:T(8,128)(2,1)S(1)}, bf16[128,1024]{1,0:T(8,128)(2,1)S(1)}, u32[]{:S(2)}, u32[]{:S(2)}) %collective-permute-start.1) | collective-permute-done | bytes 262176 | tf_op jit(solution)/shard_map/ppermute | solution.py:21
  16.1 1.4 %collective-permute-start.5 = (bf16[128,1024]{1,0:T(8,128)(2,1)S(1)}, bf16[128,1024]{1,0:T(8,128)(2,1)S(1)}, u32[]{:S(2)}, u32[]{:S(2)}) collective-permute-start(bf16[128,1024]{1,0:T(8,128)(2,1)S(1)} %collective-permute-done.3.down_low.refs_2_), channel_id=1, source_target_pairs={{0,3},{1,0},{2,1},{3,2},{4,7},{5,4},{6,5},{7,6},{8,11},{9,8},{10,9... | collective-permute-start | bytes 786440 | tf_op jit(solution)/shard_map/ppermute | solution.py:21
  17.5 3.5 %shard_map.191 = (bf16[512,1024]{1,0:T(8,128)(2,1)S(1)}, bf16[1024,512]{1,0:T(8,128)(2,1)S(1)}) custom-call(s32[1,512]{1,0:T(1,128)} %refs_0_.3, bf16[512,1024]{1,0:T(8,128)(2,1)} %refs_1_.2), custom_call_target="tpu_custom_call" | custom-call | flops 1000000000 | bytes 1050624 | tf_op jit(solution)/shard_map/pallas_call | solution.py:75
  21.0 1.8 %shard_map.194 = (f32[512,256]{1,0:T(8,128)S(1)}, f32[512,256]{1,0:T(8,128)S(1)}) custom-call(bf16[256,1024]{1,0:T(8,128)(2,1)S(1)} %copy-done.5, bf16[128,1024]{1,0:T(8,128)(2,1)S(1)} %collective-permute-done.up_top.refs_1_, bf16[128,1024]{1,0:T(8,128)(2,1)S(1)} %collective-permute-done.3.down_low.refs_2_, bf16[1024,512]{1,0:T(8,128)(2,1)S(1)} %copy-done, ...), custom_call_target="tpu_custom_call" | custom-call | flops 2000000000 | bytes 3407872 | tf_op jit(solution)/shard_map/pallas_call | solution.py:75
  22.8 3.0 %collective-permute-start.9 = (bf16[384,512]{1,0:T(8,128)(2,1)S(1)}, bf16[384,512]{1,0:T(8,128)(2,1)S(1)}, u32[]{:S(2)}, u32[]{:S(2)}) collective-permute-start(bf16[384,512]{1,0:T(8,128)(2,1)S(1)} %get-tuple-element.70.refs_0_), channel_id=1, source_target_pairs={{0,4},{4,0},{8,12},{12,8},{16,20},{20,16},{24,28},{28,24},{32,36},... | collective-permute-start | bytes 1179656 | tf_op jit(solution)/shard_map/ppermute | solution.py:16
  31.5 1.9 %collective-permute-start.13 = (bf16[256,512]{1,0:T(8,128)(2,1)S(1)}, bf16[256,512]{1,0:T(8,128)(2,1)S(1)}, u32[]{:S(2)}, u32[]{:S(2)}) collective-permute-start(bf16[256,512]{1,0:T(8,128)(2,1)S(1)} %get-tuple-element.75.refs_2_), channel_id=1, source_target_pairs={{0,24},{4,28},{8,16},{12,20},{16,8},{20,12},{24,0},{28,4},{32,56},... | collective-permute-start | bytes 786440 | tf_op jit(solution)/shard_map/ppermute | solution.py:16
  35.6 2.6 %collective-permute-start.16 = (bf16[512,128]{1,0:T(8,128)(2,1)S(1)}, bf16[512,128]{1,0:T(8,128)(2,1)S(1)}, u32[]{:S(2)}, u32[]{:S(2)}) collective-permute-start(bf16[512,128]{1,0:T(8,128)(2,1)S(1)} %get-tuple-element.83.refs_0_), channel_id=1, source_target_pairs={{0,24},{4,28},{8,16},{12,20},{16,8},{20,12},{24,0},{28,4},{32,56},... | collective-permute-start | bytes 393224 | tf_op jit(solution)/shard_map/ppermute | solution.py:16
  39.0 2.1 %collective-permute-start.12 = (bf16[512,128]{1,0:T(8,128)(2,1)S(1)}, bf16[512,128]{1,0:T(8,128)(2,1)S(1)}, u32[]{:S(2)}, u32[]{:S(2)}) collective-permute-start(bf16[512,128]{1,0:T(8,128)(2,1)S(1)} %get-tuple-element.74.refs_0_), channel_id=1, source_target_pairs={{0,24},{4,28},{8,16},{12,20},{16,8},{20,12},{24,0},{28,4},{32,56},... | collective-permute-start | bytes 393224 | tf_op jit(solution)/shard_map/ppermute | solution.py:16
  41.0 2.0 %collective-permute-done.16.refs_1_ = bf16[512,128]{1,0:T(8,128)(2,1)S(1)} collective-permute-done((bf16[512,128]{1,0:T(8,128)(2,1)S(1)}, bf16[512,128]{1,0:T(8,128)(2,1)S(1)}, u32[]{:S(2)}, u32[]{:S(2)}) %collective-permute-start.16) | collective-permute-done | bytes 131104 | tf_op jit(solution)/shard_map/ppermute | solution.py:16
  43.0 1.6 %shard_map.204 = (bf16[512,128]{1,0:T(8,128)(2,1)S(1)}, bf16[128,128]{1,0:T(8,128)(2,1)S(1)}, bf16[128,128]{1,0:T(8,128)(2,1)S(1)}, bf16[64,128]{1,0:T(8,128)(2,1)S(1)}, bf16[64,128]{1,0:T(8,128)(2,1)S(1)}) custom-call(bf16[512,128]{1,0:T(8,128)(2,1)S(1)} %get-tuple-element.83.refs_0_, bf16[512,128]{1,0:T(8,128)(2,1)S(1)} %collective-permute-done.16.refs_1_, ...), custom_call_target="tpu_custom_call" | custom-call | flops 1000000000 | bytes 3276800 | tf_op jit(solution)/shard_map/pallas_call | solution.py:75
  44.7 2.3 %collective-permute-start.17 = (bf16[512,128]{1,0:T(8,128)(2,1)S(1)}, bf16[512,128]{1,0:T(8,128)(2,1)S(1)}, u32[]{:S(2)}, u32[]{:S(2)}) collective-permute-start(bf16[512,128]{1,0:T(8,128)(2,1)S(1)} %get-tuple-element.85.s_own.first_a), channel_id=1, source_target_pairs={{0,4},{4,0},{8,12},{12,8},{16,20},{20,16},{24,28},{28,24},{32,36},... | collective-permute-start | bytes 393224 | tf_op jit(solution)/shard_map/ppermute | solution.py:16
  46.9 3.1 %shard_map.192 = (bf16[1024,512]{1,0:T(8,128)(2,1)S(1)}, bf16[3,1024,1024]{2,1,0:T(8,128)(2,1)S(1)}) custom-call(bf16[1024,512]{1,0:T(8,128)(2,1)} %refs_4_.4, bf16[3,1024,1024]{2,1,0:T(8,128)(2,1)} %surface.1), custom_call_target="tpu_custom_call" | custom-call | bytes 8388608 | tf_op jit(solution)/shard_map/pallas_call | solution.py:402
  50.1 1.6 %shard_map.193.factor = bf16[1024,1024]{1,0:T(8,128)(2,1)S(1)} custom-call(bf16[256,1024]{1,0:T(8,128)(2,1)} %refs_0_.4, bf16[128,1024]{1,0:T(8,128)(2,1)} %copy-done.6, bf16[128,1024]{1,0:T(8,128)(2,1)} %copy-done.1, bf16[128,1024]{1,0:T(8,128)(2,1)} %copy-done.2, bf16[128,1024]{1,0:T(8,128)(2,1)} %copy-done.7, bf16[128,1024]{1,0:T(8,128)(2,1)} %copy-done.3, ...), custom_call_target="tpu_custom_call" | custom-call | bytes 8388608 | tf_op jit(solution)/shard_map/pallas_call | solution.py:402
  51.7 1.7 %shard_map.202 = (bf16[512,128]{1,0:T(8,128)(2,1)S(1)}, bf16[128,128]{1,0:T(8,128)(2,1)S(1)}, bf16[128,128]{1,0:T(8,128)(2,1)S(1)}, bf16[64,128]{1,0:T(8,128)(2,1)S(1)}, bf16[64,128]{1,0:T(8,128)(2,1)S(1)}) custom-call(bf16[512,128]{1,0:T(8,128)(2,1)S(1)} %get-tuple-element.74.refs_0_, bf16[512,128]{1,0:T(8,128)(2,1)S(1)} %collective-permute-done.12.refs_1_, ...), custom_call_target="tpu_custom_call" | custom-call | flops 1000000000 | bytes 3276800 | tf_op jit(solution)/shard_map/pallas_call | solution.py:75
  53.4 4.1 %shard_map.205 = (bf16[1024,512]{1,0:T(8,128)(2,1)}, bf16[1024,256]{1,0:T(8,128)(2,1)S(1)}, bf16[1024,256]{1,0:T(8,128)(2,1)S(1)}, bf16[1024,256]{1,0:T(8,128)(2...) custom-call(bf16[1024,512]{1,0:T(8,128)(2,1)S(1)} %get-tuple-element.59.c_t, ...), custom_call_target="tpu_custom_call" | custom-call | flops 3000000000 | bytes 8388608 | tf_op jit(solution)/shard_map/pallas_call | solution.py:388
  58.1 4.1 %shard_map.206 = (bf16[1024,512]{1,0:T(8,128)(2,1)}, bf16[1024,256]{1,0:T(8,128)(2,1)S(1)}, bf16[1024,256]{1,0:T(8,128)(2,1)S(1)}, bf16[1024,256]{1,0:T(8,128)(2...) custom-call(bf16[1024,512]{1,0:T(8,128)(2,1)S(1)} %get-tuple-element.59.c_t, ...), custom_call_target="tpu_custom_call", output_to_operand_aliasing={{0}: (7, {})} | custom-call | flops 3000000000 | bytes 8388608 | tf_op jit(solution)/shard_map/pallas_call | solution.py:388
  63.5 3.2 %collective-permute-start.24 = (bf16[1024,256]{1,0:T(8,128)(2,1)S(1)}, bf16[1024,256]{1,0:T(8,128)(2,1)S(1)}, u32[]{:S(2)}, u32[]{:S(2)}) collective-permute-start(bf16[1024,256]{1,0:T(8,128)(2,1)S(1)} %get-tuple-element.100), channel_id=1, source_target_pairs={{8,16},{12,20},{16,8},{20,12},{24,32},{28,36},{32,24},{36,28},{40,... | collective-permute-start | bytes 1572872 | tf_op jit(solution)/shard_map/ppermute | solution.py:27
  67.0 5.4 %collective-permute-start.20 = (bf16[1024,256]{1,0:T(8,128)(2,1)S(1)}, bf16[1024,256]{1,0:T(8,128)(2,1)S(1)}, u32[]{:S(2)}, u32[]{:S(2)}) collective-permute-start(bf16[1024,256]{1,0:T(8,128)(2,1)S(1)} %get-tuple-element.93), channel_id=1, source_target_pairs={{8,16},{12,20},{16,8},{20,12},{24,32},{28,36},{32,24},{36,28},{40,... | collective-permute-start | bytes 1572872 | tf_op jit(solution)/shard_map/ppermute | solution.py:27
  75.8 6.1 %collective-permute-done.24.back = bf16[1024,256]{1,0:T(8,128)(2,1)S(1)} collective-permute-done((bf16[1024,256]{1,0:T(8,128)(2,1)S(1)}, bf16[1024,256]{1,0:T(8,128)(2,1)S(1)}, u32[]{:S(2)}, u32[]{:S(2)}) %collective-permute-start.24) | collective-permute-done | bytes 524320 | tf_op jit(solution)/shard_map/ppermute | solution.py:27
  82.9 10.2 %collective-permute-done.20.back = bf16[1024,256]{1,0:T(8,128)(2,1)S(1)} collective-permute-done((bf16[1024,256]{1,0:T(8,128)(2,1)S(1)}, bf16[1024,256]{1,0:T(8,128)(2,1)S(1)}, u32[]{:S(2)}, u32[]{:S(2)}) %collective-permute-start.20) | collective-permute-done | bytes 524320 | tf_op jit(solution)/shard_map/ppermute | solution.py:27
  (76 shorter events, 20.8 us)
Async XLA Ops:
  1.9 9.6 %collective-permute-start = (bf16[128,1024]{1,0:T(8,128)(2,1)S(1)}, bf16[128,1024]{1,0:T(8,128)(2,1)S(1)}, u32[]{:S(2)}, u32[]{:S(2)}) collective-permute-start(bf16[128,1024]{1,0:T(8,128)(2,1)S(1)} %get-tuple-element.114), channel_id=1, source_target_pairs={{0,1},{1,2},{2,3},{3,0},{4,5},{5,6},{6,7},{7,4},{8,9},{9,10},{10,1... | collective-permute-start | bytes 786440 | tf_op jit(solution)/shard_map/ppermute | solution.py:21
  3.2 10.8 %collective-permute-start.3 = (bf16[128,1024]{1,0:T(8,128)(2,1)S(1)}, bf16[128,1024]{1,0:T(8,128)(2,1)S(1)}, u32[]{:S(2)}, u32[]{:S(2)}) collective-permute-start(bf16[128,1024]{1,0:T(8,128)(2,1)S(1)} %get-tuple-element.113), channel_id=1, source_target_pairs={{0,3},{1,0},{2,1},{3,2},{4,7},{5,4},{6,5},{7,6},{8,11},{9,8},{10,9... | collective-permute-start | bytes 786440 | tf_op jit(solution)/shard_map/ppermute | solution.py:21
  4.8 11.3 %collective-permute-start.1 = (bf16[128,1024]{1,0:T(8,128)(2,1)S(1)}, bf16[128,1024]{1,0:T(8,128)(2,1)S(1)}, u32[]{:S(2)}, u32[]{:S(2)}) collective-permute-start(bf16[128,1024]{1,0:T(8,128)(2,1)S(1)} %get-tuple-element.113), channel_id=1, source_target_pairs={{0,1},{1,2},{2,3},{3,0},{4,5},{5,6},{6,7},{7,4},{8,9},{9,10},{10,1... | collective-permute-start | bytes 786440 | tf_op jit(solution)/shard_map/ppermute | solution.py:21
  8.4 17.4 %collective-permute-start.10 = (bf16[384,512]{1,0:T(8,128)(2,1)S(1)}, bf16[384,512]{1,0:T(8,128)(2,1)S(1)}, u32[]{:S(2)}, u32[]{:S(2)}) collective-permute-start(bf16[384,512]{1,0:T(8,128)(2,1)S(1)} %get-tuple-element.70.refs_0_), channel_id=1, source_target_pairs={{0,8},{4,12},{8,0},{12,4},{16,24},{20,28},{24,16},{28,20},{32,40},... | collective-permute-start | bytes 1179656 | tf_op jit(solution)/shard_map/ppermute | solution.py:16
  9.7 19.2 %collective-permute-start.7 = (bf16[640,512]{1,0:T(8,128)(2,1)S(1)}, bf16[640,512]{1,0:T(8,128)(2,1)S(1)}, u32[]{:S(2)}, u32[]{:S(2)}) collective-permute-start(bf16[640,512]{1,0:T(8,128)(2,1)S(1)} %get-tuple-element.65.refs_0_), channel_id=1, source_target_pairs={{0,4},{4,0},{8,12},{12,8},{16,20},{20,16},{24,28},{28,24},{32,36},... | collective-permute-start | bytes 1966088 | tf_op jit(solution)/shard_map/ppermute | solution.py:16
  11.4 11.4 %collective-permute-start.2 = (bf16[128,1024]{1,0:T(8,128)(2,1)S(1)}, bf16[128,1024]{1,0:T(8,128)(2,1)S(1)}, u32[]{:S(2)}, u32[]{:S(2)}) collective-permute-start(bf16[128,1024]{1,0:T(8,128)(2,1)S(1)} %get-tuple-element.114), channel_id=1, source_target_pairs={{0,3},{1,0},{2,1},{3,2},{4,7},{5,4},{6,5},{7,6},{8,11},{9,8},{10,9... | collective-permute-start | bytes 786440 | tf_op jit(solution)/shard_map/ppermute | solution.py:21
  14.0 11.9 %collective-permute-start.4 = (bf16[128,1024]{1,0:T(8,128)(2,1)S(1)}, bf16[128,1024]{1,0:T(8,128)(2,1)S(1)}, u32[]{:S(2)}, u32[]{:S(2)}) collective-permute-start(bf16[128,1024]{1,0:T(8,128)(2,1)S(1)} %collective-permute-done.up_top.refs_1_), channel_id=1, source_target_pairs={{0,1},{1,2},{2,3},{3,0},{4,5},{5,6},{6,7},{7,4},{8,9},{9,10},{10,1... | collective-permute-start | bytes 786440 | tf_op jit(solution)/shard_map/ppermute | solution.py:21
  16.1 9.9 %collective-permute-start.5 = (bf16[128,1024]{1,0:T(8,128)(2,1)S(1)}, bf16[128,1024]{1,0:T(8,128)(2,1)S(1)}, u32[]{:S(2)}, u32[]{:S(2)}) collective-permute-start(bf16[128,1024]{1,0:T(8,128)(2,1)S(1)} %collective-permute-done.3.down_low.refs_2_), channel_id=1, source_target_pairs={{0,3},{1,0},{2,1},{3,2},{4,7},{5,4},{6,5},{7,6},{8,11},{9,8},{10,9... | collective-permute-start | bytes 786440 | tf_op jit(solution)/shard_map/ppermute | solution.py:21
  22.8 8.4 %collective-permute-start.9 = (bf16[384,512]{1,0:T(8,128)(2,1)S(1)}, bf16[384,512]{1,0:T(8,128)(2,1)S(1)}, u32[]{:S(2)}, u32[]{:S(2)}) collective-permute-start(bf16[384,512]{1,0:T(8,128)(2,1)S(1)} %get-tuple-element.70.refs_0_), channel_id=1, source_target_pairs={{0,4},{4,0},{8,12},{12,8},{16,20},{20,16},{24,28},{28,24},{32,36},... | collective-permute-start | bytes 1179656 | tf_op jit(solution)/shard_map/ppermute | solution.py:16
  25.8 5.4 %collective-permute-start.11 = (bf16[384,512]{1,0:T(8,128)(2,1)S(1)}, bf16[384,512]{1,0:T(8,128)(2,1)S(1)}, u32[]{:S(2)}, u32[]{:S(2)}) collective-permute-start(bf16[384,512]{1,0:T(8,128)(2,1)S(1)} %collective-permute-done.10.refs_2_), channel_id=1, source_target_pairs={{0,4},{4,0},{8,12},{12,8},{16,20},{20,16},{24,28},{28,24},{32,36},... | collective-permute-start | bytes 1179656 | tf_op jit(solution)/shard_map/ppermute | solution.py:16
  29.9 5.0 %collective-permute-start.15 = (bf16[512,128]{1,0:T(8,128)(2,1)S(1)}, bf16[512,128]{1,0:T(8,128)(2,1)S(1)}, u32[]{:S(2)}, u32[]{:S(2)}) collective-permute-start(bf16[512,128]{1,0:T(8,128)(2,1)S(1)} %get-tuple-element.82.refs_0_), channel_id=1, source_target_pairs={{0,8},{4,12},{8,0},{12,4},{16,24},{20,28},{24,16},{28,20},{32,40},... | collective-permute-start | bytes 393224 | tf_op jit(solution)/shard_map/ppermute | solution.py:16
  31.5 11.5 %collective-permute-start.13 = (bf16[256,512]{1,0:T(8,128)(2,1)S(1)}, bf16[256,512]{1,0:T(8,128)(2,1)S(1)}, u32[]{:S(2)}, u32[]{:S(2)}) collective-permute-start(bf16[256,512]{1,0:T(8,128)(2,1)S(1)} %get-tuple-element.75.refs_2_), channel_id=1, source_target_pairs={{0,24},{4,28},{8,16},{12,20},{16,8},{20,12},{24,0},{28,4},{32,56},... | collective-permute-start | bytes 786440 | tf_op jit(solution)/shard_map/ppermute | solution.py:16
  33.4 4.8 %collective-permute-start.8 = (bf16[512,128]{1,0:T(8,128)(2,1)S(1)}, bf16[512,128]{1,0:T(8,128)(2,1)S(1)}, u32[]{:S(2)}, u32[]{:S(2)}) collective-permute-start(bf16[512,128]{1,0:T(8,128)(2,1)S(1)} %get-tuple-element.69.refs_0_), channel_id=1, source_target_pairs={{0,8},{4,12},{8,0},{12,4},{16,24},{20,28},{24,16},{28,20},{32,40},... | collective-permute-start | bytes 393224 | tf_op jit(solution)/shard_map/ppermute | solution.py:16
  35.6 7.4 %collective-permute-start.16 = (bf16[512,128]{1,0:T(8,128)(2,1)S(1)}, bf16[512,128]{1,0:T(8,128)(2,1)S(1)}, u32[]{:S(2)}, u32[]{:S(2)}) collective-permute-start(bf16[512,128]{1,0:T(8,128)(2,1)S(1)} %get-tuple-element.83.refs_0_), channel_id=1, source_target_pairs={{0,24},{4,28},{8,16},{12,20},{16,8},{20,12},{24,0},{28,4},{32,56},... | collective-permute-start | bytes 393224 | tf_op jit(solution)/shard_map/ppermute | solution.py:16
  39.0 12.7 %collective-permute-start.12 = (bf16[512,128]{1,0:T(8,128)(2,1)S(1)}, bf16[512,128]{1,0:T(8,128)(2,1)S(1)}, u32[]{:S(2)}, u32[]{:S(2)}) collective-permute-start(bf16[512,128]{1,0:T(8,128)(2,1)S(1)} %get-tuple-element.74.refs_0_), channel_id=1, source_target_pairs={{0,24},{4,28},{8,16},{12,20},{16,8},{20,12},{24,0},{28,4},{32,56},... | collective-permute-start | bytes 393224 | tf_op jit(solution)/shard_map/ppermute | solution.py:16
  44.7 8.8 %collective-permute-start.17 = (bf16[512,128]{1,0:T(8,128)(2,1)S(1)}, bf16[512,128]{1,0:T(8,128)(2,1)S(1)}, u32[]{:S(2)}, u32[]{:S(2)}) collective-permute-start(bf16[512,128]{1,0:T(8,128)(2,1)S(1)} %get-tuple-element.85.s_own.first_a), channel_id=1, source_target_pairs={{0,4},{4,0},{8,12},{12,8},{16,20},{20,16},{24,28},{28,24},{32,36},... | collective-permute-start | bytes 393224 | tf_op jit(solution)/shard_map/ppermute | solution.py:16
  53.3 4.8 %collective-permute-start.14 = (bf16[512,128]{1,0:T(8,128)(2,1)S(1)}, bf16[512,128]{1,0:T(8,128)(2,1)S(1)}, u32[]{:S(2)}, u32[]{:S(2)}) collective-permute-start(bf16[512,128]{1,0:T(8,128)(2,1)S(1)} %get-tuple-element.80.s_own.first_b), channel_id=1, source_target_pairs={{0,4},{4,0},{8,12},{12,8},{16,20},{20,16},{24,28},{28,24},{32,36},... | collective-permute-start | bytes 393224 | tf_op jit(solution)/shard_map/ppermute | solution.py:16
  57.5 5.9 %collective-permute-start.23 = (bf16[1024,256]{1,0:T(8,128)(2,1)S(1)}, bf16[1024,256]{1,0:T(8,128)(2,1)S(1)}, u32[]{:S(2)}, u32[]{:S(2)}) collective-permute-start(bf16[1024,256]{1,0:T(8,128)(2,1)S(1)} %get-tuple-element.99), channel_id=1, source_target_pairs={{0,4},{4,0},{8,12},{12,8},{16,20},{20,16},{24,28},{28,24},{32,36},... | collective-permute-start | bytes 1572872 | tf_op jit(solution)/shard_map/ppermute | solution.py:16
  62.3 10.1 %collective-permute-start.22 = (bf16[1024,256]{1,0:T(8,128)(2,1)S(1)}, bf16[1024,256]{1,0:T(8,128)(2,1)S(1)}, u32[]{:S(2)}, u32[]{:S(2)}) collective-permute-start(bf16[1024,256]{1,0:T(8,128)(2,1)S(1)} %get-tuple-element.96), channel_id=1, source_target_pairs={{0,4},{4,0},{8,12},{12,8},{16,20},{20,16},{24,28},{28,24},{32,36},... | collective-permute-start | bytes 1572872 | tf_op jit(solution)/shard_map/ppermute | solution.py:16
  63.0 19.9 %collective-permute-start.18 = (bf16[1024,256]{1,0:T(8,128)(2,1)S(1)}, bf16[1024,256]{1,0:T(8,128)(2,1)S(1)}, u32[]{:S(2)}, u32[]{:S(2)}) collective-permute-start(bf16[1024,256]{1,0:T(8,128)(2,1)S(1)} %get-tuple-element.89), channel_id=1, source_target_pairs={{0,4},{4,0},{8,12},{12,8},{16,20},{20,16},{24,28},{28,24},{32,36},... | collective-permute-start | bytes 1572872 | tf_op jit(solution)/shard_map/ppermute | solution.py:16
  63.5 18.4 %collective-permute-start.24 = (bf16[1024,256]{1,0:T(8,128)(2,1)S(1)}, bf16[1024,256]{1,0:T(8,128)(2,1)S(1)}, u32[]{:S(2)}, u32[]{:S(2)}) collective-permute-start(bf16[1024,256]{1,0:T(8,128)(2,1)S(1)} %get-tuple-element.100), channel_id=1, source_target_pairs={{8,16},{12,20},{16,8},{20,12},{24,32},{28,36},{32,24},{36,28},{40,... | collective-permute-start | bytes 1572872 | tf_op jit(solution)/shard_map/ppermute | solution.py:27
  66.8 15.1 %collective-permute-start.25 = (bf16[1024,256]{1,0:T(8,128)(2,1)S(1)}, bf16[1024,256]{1,0:T(8,128)(2,1)S(1)}, u32[]{:S(2)}, u32[]{:S(2)}) collective-permute-start(bf16[1024,256]{1,0:T(8,128)(2,1)S(1)} %get-tuple-element.101), channel_id=1, source_target_pairs={{0,8},{4,12},{8,0},{12,4},{16,24},{20,28},{24,16},{28,20},{32,40},... | collective-permute-start | bytes 1572872 | tf_op jit(solution)/shard_map/ppermute | solution.py:16
  67.0 26.1 %collective-permute-start.20 = (bf16[1024,256]{1,0:T(8,128)(2,1)S(1)}, bf16[1024,256]{1,0:T(8,128)(2,1)S(1)}, u32[]{:S(2)}, u32[]{:S(2)}) collective-permute-start(bf16[1024,256]{1,0:T(8,128)(2,1)S(1)} %get-tuple-element.93), channel_id=1, source_target_pairs={{8,16},{12,20},{16,8},{20,12},{24,32},{28,36},{32,24},{36,28},{40,... | collective-permute-start | bytes 1572872 | tf_op jit(solution)/shard_map/ppermute | solution.py:27
  72.4 20.7 %collective-permute-start.21 = (bf16[1024,256]{1,0:T(8,128)(2,1)S(1)}, bf16[1024,256]{1,0:T(8,128)(2,1)S(1)}, u32[]{:S(2)}, u32[]{:S(2)}) collective-permute-start(bf16[1024,256]{1,0:T(8,128)(2,1)S(1)} %get-tuple-element.94), channel_id=1, source_target_pairs={{0,8},{4,12},{8,0},{12,4},{16,24},{20,28},{24,16},{28,20},{32,40},... | collective-permute-start | bytes 1572872 | tf_op jit(solution)/shard_map/ppermute | solution.py:16
  (13 other events, 135.0 us)
